TPU v7x, 32 devices: a whole 2x2x4 slice. The times are simulated.
32 devices in a mesh: tm: 4 (over y, x), tile: 8 (over z, core).
Axes of the slice: x: 2, y: 2, z: 4, core: 2. Of those that a mesh axis runs over, the one named last changes fastest.
Arguments:
- diag_blocks: float32 [16384, 4096], P(('tm', 'tile')), as said below
- coupling: float32 [16384, 4096], P(('tm', 'tile')), as said below
- next_diag: float32 [16384, 4096], P(('tm', 'tile')), as said below
- arrow_now: float32 [128, 4096], P('tm'), may hold values from -0.4375 to 0.4375
- arrow_next: float32 [128, 4096], P('tm'), may hold values from -0.4375 to 0.4375
- arrow_tip: float32 [128, 32], P('tm'), may hold values from -6 to 6
Outputs:
- factor_lower: float32 [16384, 4096], P(('tm', 'tile'))
- coupling_out: float32 [16384, 4096], P(('tm', 'tile'))
- arrow_factor: float32 [128, 4096], P('tm')
- handed_diag: float32 [16384, 4096], P(('tm', 'tile'))
- handed_arrow: float32 [128, 4096], P('tm')
- handed_tip: float32 [128, 32], P('tm')
Inputs may be any that keep to these rules, and one draw needn't show every extreme that they name: `diag_blocks`: each 4096 x 4096 block is symmetric positive definite. `next_diag`: each 4096 x 4096 block is symmetric positive definite. `coupling`: with the diag_blocks block and the next_diag block of its time step, each 4096 x 4096 block forms a symmetric positive definite two-block precision matrix.
All inputs are finite; a program needn't handle non-finite values.
Results may differ from a plain program's by a relative error of at most 0.0001.
Values sent between devices are 32-bit elements; how exact they have to be, the bound alone decides.
No kernel may reach another device: no remote copies, remote signals or barrier semaphores. Data moves between devices by JAX's collectives and lax.ppermute only.
A program may use at most 256 MiB of HBM per device.

v0:
```python
import jax
import jax.numpy as jnp
from jax import lax
from jax.sharding import PartitionSpec as P

precise = lax.Precision.HIGHEST


def broadcast(block, axis, source):
    block = jnp.where(lax.axis_index(axis) == source, block, jnp.zeros_like(block))
    return lax.psum(block, axis)


def shifted(value, axis, steps):
    count = lax.axis_size(axis)
    leading, last = (max(0, -steps), min(count, count - steps))
    return lax.ppermute(value, axis, [(source, source + steps) for source in range(leading, last)])


def outer_rows(left_rows, right_rows):
    return lax.dot_general(
        left_rows,
        right_rows,
        (((1,), (1,)), ((), ())),
        precision=precise,
        preferred_element_type=jnp.float32,
    )


def solve_rows(factor, block):
    return jax.scipy.linalg.solve_triangular(factor, block.T, lower=True).T


def local(diag_blocks, coupling, next_diag, arrow_now, arrow_next, arrow_tip):
    row_count = diag_blocks.shape[0]
    col_count = diag_blocks.shape[1]
    panels = lax.axis_size("tile") // 4
    my_index = lax.axis_index("tile")
    row_ids = my_index * row_count + lax.iota(jnp.int32, row_count)
    work_a, work_c, arrow_a = (diag_blocks, coupling, arrow_now)
    next_d, arrow_b, tip_block = (next_diag, arrow_next, arrow_tip)
    for number in range(panels):
        offset = number * row_count
        factor_offset = number * row_count
        factor_ending = factor_offset + row_count
        pivot_blk = broadcast(work_a[:, factor_offset:factor_ending], "tile", number)
        factor = jnp.linalg.cholesky(pivot_blk)
        factor_local_a = jnp.where(
            (row_ids >= factor_offset)[:, None],
            solve_rows(factor, work_a[:, factor_offset:factor_ending]),
            0.0,
        )
        factor_local_c = solve_rows(factor, work_c[:, factor_offset:factor_ending])
        factor_whole_a = lax.all_gather(factor_local_a, "tile", axis=0, tiled=True)
        factor_whole_c = lax.all_gather(factor_local_c, "tile", axis=0, tiled=True)
        factor_local_r = solve_rows(factor, arrow_a[:, factor_offset:factor_ending])
        panel_k = (
            factor_offset,
            factor_local_a,
            factor_local_c,
            factor_local_r,
            factor_whole_a,
            factor_whole_c,
        )
        store_work_a = work_a
        store_work_c = work_c
        store_arrow_a = arrow_a
        store_offset = panel_k[0]
        store_local_a = panel_k[1]
        store_local_c = panel_k[2]
        store_local_r = panel_k[3]
        ending = store_offset + row_count
        store_work_a = store_work_a.at[:, store_offset:ending].set(store_local_a)
        store_work_c = store_work_c.at[:, store_offset:ending].set(store_local_c)
        store_arrow_a = store_arrow_a.at[:, store_offset:ending].set(store_local_r)
        work_a = store_work_a
        work_c = store_work_c
        arrow_a = store_arrow_a
        col_lo = offset + row_count
        apply_work_a = work_a
        apply_work_c = work_c
        apply_arrow_a = arrow_a
        apply_offset = panel_k[0]
        local_a = panel_k[1]
        apply_local_c = panel_k[2]
        apply_local_r = panel_k[3]
        whole_a = panel_k[4]
        keep_rows = (row_ids >= apply_offset + row_count)[:, None]
        targets = whole_a[col_lo:col_count]
        apply_work_a = apply_work_a.at[:, col_lo:col_count].add(
            -jnp.where(keep_rows, outer_rows(local_a, targets), 0.0)
        )
        apply_work_c = apply_work_c.at[:, col_lo:col_count].add(-outer_rows(apply_local_c, targets))
        apply_arrow_a = apply_arrow_a.at[:, col_lo:col_count].add(
            -outer_rows(apply_local_r, targets)
        )
        work_a = apply_work_a
        work_c = apply_work_c
        arrow_a = apply_arrow_a
        apply_next_d = next_d
        apply_arrow_b = arrow_b
        apply_tip_block = tip_block
        local_c = panel_k[2]
        local_r = panel_k[3]
        whole_c = panel_k[5]
        apply_next_d = apply_next_d - outer_rows(local_c, whole_c)
        apply_arrow_b = apply_arrow_b - outer_rows(local_r, whole_c)
        apply_tip_block = apply_tip_block - outer_rows(local_r, local_r)
        next_d = apply_next_d
        arrow_b = apply_arrow_b
        tip_block = apply_tip_block
    col_ids = lax.iota(jnp.int32, col_count)
    factor_lower = jnp.where(col_ids[None, :] <= row_ids[:, None], work_a, 0.0)
    handed_diag, handed_arrow, handed_tip = shifted((next_d, arrow_b, tip_block), "tm", 1)
    return (factor_lower, work_c, arrow_a, handed_diag, handed_arrow, handed_tip)


def solution(mesh):
    return jax.shard_map(
        local,
        mesh=mesh,
        in_specs=(
            P(("tm", "tile"), None),
            P(("tm", "tile"), None),
            P(("tm", "tile"), None),
            P("tm", None),
            P("tm", None),
            P("tm", None),
        ),
        out_specs=(
            P(("tm", "tile"), None),
            P(("tm", "tile"), None),
            P("tm", None),
            P(("tm", "tile"), None),
            P("tm", None),
            P("tm", None),
        ),
        check_vma=False,
    )
```

profile of v0, /device:TPU:19, one launch (start us, length us, event | category | flops | bytes accessed | tf_op | source)
XLA Modules:
  0.0 910.7 jit_solution(8446192928893483997)
XLA Ops:
  22.5 56.1 %all-reduce.4.cloned.1.call-done = f32[512,512]{1,0:T(8,128)} async-done(((f32[512,512]{1,0:T(8,128)}), f32[512,512]{1,0:T(8,128)}) %all-reduce.4.cloned.1.call-update) | async-done | bytes 1048592 | tf_op jit(solution)/shard_map/psum | solution.py:11
  81.8 11.7 %cholesky.286 = f32[128,128]{1,0:T(8,128)S(1)} custom-call(f32[128,128]{1,0:T(8,128)S(1)} %copy.14), custom_call_target="Cholesky" | custom-call | tf_op jit(solution)/shard_map/jit(cholesky)/cholesky | solution.py:47
  104.5 11.7 %cholesky.305 = f32[128,128]{1,0:T(8,128)S(1)} custom-call(f32[128,128]{1,0:T(8,128)S(1)} %copy.16), custom_call_target="Cholesky" | custom-call | tf_op jit(solution)/shard_map/jit(cholesky)/cholesky | solution.py:47
  116.3 10.0 %custom-call.34 = f32[1,128,128]{1,2,0:T(8,128)S(1)} custom-call(f32[1,128,128]{2,1,0:T(8,128)S(1)} %get-tuple-element.243), custom_call_target="InvertDiagBlocksLowerTriangular" | custom-call | tf_op jit(solution)/shard_map/jit(cholesky)/cholesky | solution.py:47
  127.2 11.7 %cholesky.326 = f32[128,128]{1,0:T(8,128)S(1)} custom-call(f32[128,128]{1,0:T(8,128)S(1)} %copy.18), custom_call_target="Cholesky" | custom-call | tf_op jit(solution)/shard_map/jit(cholesky)/cholesky | solution.py:47
  150.2 12.2 %cholesky.343 = f32[128,128]{1,0:T(8,128)S(1)} custom-call(f32[128,128]{1,0:T(8,128)S(1)} %copy.20), custom_call_target="Cholesky" | custom-call | tf_op jit(solution)/shard_map/jit(cholesky)/cholesky | solution.py:47
  174.1 39.3 %custom-call.36 = f32[4,128,128]{1,2,0:T(8,128)S(1)} custom-call(f32[4,128,128]{2,1,0:T(8,128)S(1)} %get-tuple-element.193), custom_call_target="InvertDiagBlocksLowerTriangular" | custom-call | tf_op jit(solution)/shard_map/jit(_solve_triangular)/triangular_solve | solution.py:31
  232.7 76.0 %all-gather.5.cloned.1.call-done = f32[4096,512]{1,0:T(8,128)} async-done(((f32[512,512]{1,0:T(8,128)}), f32[4096,512]{1,0:T(8,128)}) %all-gather.5.cloned.1.call-update) | async-done | bytes 8388624 | tf_op jit(solution)/shard_map/all_gather | solution.py:54
  308.7 17.8 %constant_dynamic-update-slice_fusion.4 = (f32[512,4096]{1,0:T(8,128)}, f32[512,3584]{1,0:T(8,128)S(1)}) fusion(f32[512,4096]{1,0:T(8,128)} %get-tuple-element.217, f32[4096,512]{1,0:T(8,128)} %all-gather.5.cloned.1.call-done, f32[128,512]{0,1:T(8,128)} %copy-done.17, f32[128,512]{0,1:T(8,128)} %copy-done.16, f32[128,512]{0,1:T(8,128)} %copy-done.15, ...), kind=kOutput, calls=%fused_computation.244 | convolution fusion | flops 11280842752 | bytes 30409728 | tf_op jit(solution)/shard_map/dot_general | solution.py:21
  341.4 17.6 %constant_dynamic-update-slice_fusion.3 = (f32[512,4096]{1,0:T(8,128)}, f32[512,3584]{1,0:T(8,128)S(1)}) fusion(f32[512,4096]{1,0:T(8,128)} %select_dynamic-update-slice_fusion.1, f32[4096,512]{1,0:T(8,128)} %all-gather.5.cloned.1.call-done, f32[128,512]{0,1:T(8,128)S(1)} %fusion.130, f32[128,512]{0,1:T(8,128)S(1)} %copy.33, f32[128,512]{0,1:T(8,128)S(1)} %copy.32, ...), kind=kOutput, calls=%fused_computation.243 | convolution fusion | flops 11278745600 | bytes 30408704 | tf_op jit(solution)/shard_map/dot_general | solution.py:21
  363.0 26.7 %all-reduce.6.cloned.1.call-done = f32[512,512]{0,1:T(8,128)} async-done(((f32[512,512]{0,1:T(8,128)}), f32[512,512]{0,1:T(8,128)}) %all-reduce.6.cloned.1.call-update) | async-done | bytes 1048592 | tf_op jit(solution)/shard_map/psum | solution.py:11
  393.7 11.7 %cholesky.358 = f32[128,128]{1,0:T(8,128)S(1)} custom-call(f32[128,128]{1,0:T(8,128)S(1)} %cholesky.439), custom_call_target="Cholesky" | custom-call | tf_op jit(solution)/shard_map/jit(cholesky)/cholesky | solution.py:47
  418.6 11.7 %cholesky.377 = f32[128,128]{1,0:T(8,128)S(1)} custom-call(f32[128,128]{1,0:T(8,128)S(1)} %cholesky.443), custom_call_target="Cholesky" | custom-call | tf_op jit(solution)/shard_map/jit(cholesky)/cholesky | solution.py:47
  430.3 9.9 %custom-call.38 = f32[1,128,128]{1,2,0:T(8,128)S(1)} custom-call(f32[1,128,128]{2,1,0:T(8,128)S(1)} %get-tuple-element.233), custom_call_target="InvertDiagBlocksLowerTriangular" | custom-call | tf_op jit(solution)/shard_map/jit(cholesky)/cholesky | solution.py:47
  442.7 11.7 %cholesky.398 = f32[128,128]{1,0:T(8,128)S(1)} custom-call(f32[128,128]{1,0:T(8,128)S(1)} %cholesky.448), custom_call_target="Cholesky" | custom-call | tf_op jit(solution)/shard_map/jit(cholesky)/cholesky | solution.py:47
  465.7 11.7 %cholesky.415 = f32[128,128]{1,0:T(8,128)S(1)} custom-call(f32[128,128]{1,0:T(8,128)S(1)} %convolution_subtract_fusion.18), custom_call_target="Cholesky" | custom-call | tf_op jit(solution)/shard_map/jit(cholesky)/cholesky | solution.py:47
  484.1 11.9 %while.25 = (s32[]{:T(128)}, f32[512,512]{1,0:T(8,128)}, s32[4,2]{0,1:T(2,128)S(1)}, f32[4,128,128]{2,1,0:T(8,128)S(1)}, s32[]{:T(128)}) while((s32[]{:T(128)}, f32[512,512]{1,0:T(8,128)}, s32[4,2]{0,1:T(2,128)S(1)}, f32[4,128,128]{2,1,0:T(8,128)S(1)}, s32[]{:T(128)}) %tuple.143), condition=%wide.while_cond.12.clone, body=%wide.while_body.12.clone.sunk | while | flops 2 | bytes 131189 | solution.py:31
  496.0 39.3 %custom-call.40 = f32[4,128,128]{1,2,0:T(8,128)S(1)} custom-call(f32[4,128,128]{2,1,0:T(8,128)S(1)} %get-tuple-element.194), custom_call_target="InvertDiagBlocksLowerTriangular" | custom-call | tf_op jit(solution)/shard_map/jit(_solve_triangular)/triangular_solve | solution.py:31
  575.0 17.3 %fusion.92 = f32[512,4096]{1,0:T(8,128)} fusion(f32[4096,512]{1,0:T(8,128)} %all-gather.9.cloned.1.call-done, f32[128,512]{0,1:T(8,128)S(1)} %fusion.130, f32[128,512]{0,1:T(8,128)S(1)} %copy.33, f32[128,512]{0,1:T(8,128)S(1)} %copy.32, f32[128,512]{0,1:T(8,128)S(1)} %copy.31), kind=kOutput, calls=%fused_computation.136 | convolution fusion | flops 12885688320 | bytes 17825792 | tf_op jit(solution)/shard_map/dot_general | solution.py:21
  592.3 39.2 %all-gather.11.cloned.1.call-done = f32[4096,512]{1,0:T(8,128)} async-done(((f32[512,512]{1,0:T(8,128)}), f32[4096,512]{1,0:T(8,128)}) %all-gather.11.cloned.1.call-update) | async-done | bytes 8388624 | tf_op jit(solution)/shard_map/all_gather | solution.py:55
  631.5 21.0 %subtract_subtract_fusion = f32[512,4096]{1,0:T(8,128)} fusion(f32[512,4096]{1,0:T(8,128)} %param.37, f32[512,4096]{1,0:T(8,128)} %fusion.92, f32[4096,512]{1,0:T(8,128)} %all-gather.11.cloned.1.call-done, f32[128,512]{0,1:T(8,128)S(1)} %fusion.140, f32[128,512]{0,1:T(8,128)S(1)} %copy.37, f32[128,512]{0,1:T(8,128)S(1)} %copy.36, f32[128,512]{0,1:T(8,128)S(1)} %copy.35), kind=kOutput, calls=%fused_computation.4 | convolution fusion | flops 12889882624 | bytes 34603008 | tf_op jit(solution)/shard_map/dot_general | solution.py:21
  686.0 151.1 %collective-permute-done.2 = f32[32,32]{1,0:T(8,128)S(1)} collective-permute-done((f32[32,32]{1,0:T(8,128)S(1)}, f32[32,32]{1,0:T(8,128)S(1)}, u32[]{:S(2)}, u32[]{:S(2)}) %collective-permute-start.2) | collective-permute-done | bytes 4128 | tf_op jit(solution)/shard_map/ppermute | solution.py:17
  849.1 15.2 %fusion.7 = f32[512,4096]{1,0:T(8,128)} fusion(f32[512,4096]{1,0:T(8,128)} %get-tuple-element.215, f32[4096,512]{1,0:T(8,128)} %all-gather.7.cloned.1.call-done, pred[512]{0:T(512)(128)(4,1)S(1)} %fusion.166, f32[128,512]{0,1:T(8,128)S(1)} %copy-done.13, f32[128,512]{0,1:T(8,128)S(1)} %copy-done.11, f32[128,512]{0,1:T(8,128)S(1)} %copy-done.10, ...), kind=kOutput, calls=%fused_computation.17 | convolution fusion | flops 9669443584 | bytes 19923968 | tf_op jit(solution)/shard_map/dot_general | solution.py:21
  873.0 14.0 %fusion.6 = f32[512,4096]{1,0:T(8,128)} fusion(f32[512,4096]{1,0:T(8,128)} %select_dynamic-update-slice_fusion, f32[4096,512]{1,0:T(8,128)S(1)} %copy-done, f32[128,512]{0,1:T(8,128)S(1)} %fusion.140, f32[128,512]{0,1:T(8,128)S(1)} %copy.37, f32[128,512]{0,1:T(8,128)S(1)} %copy.36, f32[128,512]{0,1:T(8,128)S(1)} %copy.35), kind=kOutput, calls=%fused_computation.15 | convolution fusion | flops 9667608576 | bytes 19922944 | tf_op jit(solution)/shard_map/dot_general | solution.py:21
  (246 shorter events, 252.5 us)
Async XLA Ops:
  7.2 71.5 %all-reduce.4.cloned.1.call-start = ((), (), s32[]{:S(2)}) async-start(), calls=%async_computation | async-start | bytes 2097152 | tf_op jit(solution)/shard_map/psum | solution.py:11
  21.8 286.9 %all-gather.5.cloned.1.call-start = ((), (), s32[]{:S(2)}) async-start(), calls=%async_computation.1 | async-start | bytes 9437184 | tf_op jit(solution)/shard_map/all_gather | solution.py:54
  214.0 11.5 %copy-start.14 = (f32[128,512]{0,1:T(8,128)}, f32[128,512]{0,1:T(8,128)S(1)}, u32[]{:S(2)}) copy-start(f32[128,512]{0,1:T(8,128)S(1)} %copy.21) | copy-start | bytes 786436
  215.1 10.4 %copy-start.15 = (f32[128,512]{0,1:T(8,128)}, f32[128,512]{0,1:T(8,128)S(1)}, u32[]{:S(2)}) copy-start(f32[128,512]{0,1:T(8,128)S(1)} %copy.22) | copy-start | bytes 786436
  225.5 164.2 %all-reduce.6.cloned.1.call-start = ((), (), s32[]{:S(2)}) async-start(), calls=%async_computation.2 | async-start | bytes 2097152 | tf_op jit(solution)/shard_map/psum | solution.py:11
  226.9 99.7 %copy-start.7 = (f32[512,512]{0,1:T(8,128)}, f32[512,512]{0,1:T(8,128)S(1)}, u32[]{:S(2)}) copy-start(f32[512,512]{0,1:T(8,128)S(1)} %slice_bitcast_fusion.1) | copy-start | bytes 3145732
  333.4 241.5 %all-gather.9.cloned.1.call-start = ((), (), s32[]{:S(2)}) async-start(), calls=%async_computation.4 | async-start | bytes 9437184 | tf_op jit(solution)/shard_map/all_gather | solution.py:55
  338.3 293.2 %all-gather.11.cloned.1.call-start = ((), (), s32[]{:S(2)}) async-start(), calls=%async_computation.5 | async-start | bytes 9437184 | tf_op jit(solution)/shard_map/all_gather | solution.py:55
  548.3 300.8 %all-gather.7.cloned.1.call-start = ((), (), s32[]{:S(2)}) async-start(), calls=%async_computation.3 | async-start | bytes 9437184 | tf_op jit(solution)/shard_map/all_gather | solution.py:54
  592.3 64.6 %copy-start.26 = (f32[32,32]{1,0:T(8,128)S(1)}, f32[32,32]{1,0:T(8,128)}, u32[]{:S(2)}) copy-start(f32[32,32]{1,0:T(8,128)} %param.40) | copy-start | bytes 12292
  592.3 64.8 %copy-start.5 = (f32[32,4096]{1,0:T(8,128)S(1)}, f32[32,4096]{1,0:T(8,128)}, u32[]{:S(2)}) copy-start(f32[32,4096]{1,0:T(8,128)} %copy.107) | copy-start | bytes 1572868
  652.5 14.5 %copy-start.1 = (f32[4096,512]{1,0:T(8,128)S(1)}, f32[4096,512]{1,0:T(8,128)}, u32[]{:S(2)}) copy-start(f32[4096,512]{1,0:T(8,128)} %all-gather.9.cloned.1.call-done) | copy-start | bytes 25165828
  652.5 14.5 %copy-start.24 = (f32[32,4096]{1,0:T(8,128)S(1)}, f32[32,4096]{1,0:T(8,128)}, u32[]{:S(2)}) copy-start(f32[32,4096]{1,0:T(8,128)} %param.39) | copy-start | bytes 1572868
  652.5 240.4 %collective-permute-start = (f32[512,4096]{1,0:T(8,128)}, f32[512,4096]{1,0:T(8,128)}, u32[]{:S(2)}, u32[]{:S(2)}) collective-permute-start(f32[512,4096]{1,0:T(8,128)} %subtract_subtract_fusion), channel_id=1, source_target_pairs={{0,8},{8,16},{16,24},{1,9},{9,17},{17,25},{2,10},{10,18},{18,26},{... | collective-permute-start | bytes 25165832 | tf_op jit(solution)/shard_map/ppermute | solution.py:17
  657.8 16.9 %copy-start.21 = (f32[4,128,128]{1,2,0:T(8,128)S(1)}, f32[4,128,128]{1,2,0:T(8,128)}, u32[]{:S(2)}) copy-start(f32[4,128,128]{1,2,0:T(8,128)} %copy-done.20) | copy-start | bytes 786436
  657.8 179.3 %slice-start = ((s8[8388608]{0:T(1024)(128)(4,1)}), s8[4194304]{0:T(1024)(128)(4,1)S(1)}, s32[]{:S(2)}) async-start(s8[8388608]{0:T(1024)(128)(4,1)} %bitcast.194), calls=%async_computation.6 | async-start | bytes 8388608
  667.1 170.1 %slice-start.1 = ((s8[8388608]{0:T(1024)(128)(4,1)}), s8[4194304]{0:T(1024)(128)(4,1)S(1)}, s32[]{:S(2)}) async-start(s8[8388608]{0:T(1024)(128)(4,1)} %bitcast.194), calls=%async_computation.7 | async-start | bytes 8388608
  674.7 174.3 %copy-start.9 = (f32[128,512]{0,1:T(8,128)S(1)}, f32[128,512]{0,1:T(8,128)}, u32[]{:S(2)}) copy-start(f32[128,512]{0,1:T(8,128)} %copy.27) | copy-start | bytes 786436
  674.7 174.3 %copy-start.10 = (f32[128,512]{0,1:T(8,128)S(1)}, f32[128,512]{0,1:T(8,128)}, u32[]{:S(2)}) copy-start(f32[128,512]{0,1:T(8,128)} %copy.28) | copy-start | bytes 786436
  674.7 174.3 %copy-start.11 = (f32[128,512]{0,1:T(8,128)S(1)}, f32[128,512]{0,1:T(8,128)}, u32[]{:S(2)}) copy-start(f32[128,512]{0,1:T(8,128)} %copy.29) | copy-start | bytes 786436
  674.7 174.3 %copy-start.13 = (f32[128,512]{0,1:T(8,128)S(1)}, f32[128,512]{0,1:T(8,128)}, u32[]{:S(2)}) copy-start(f32[128,512]{0,1:T(8,128)} %copy-done.12) | copy-start | bytes 786436
  679.2 157.9 %collective-permute-start.2 = (f32[32,32]{1,0:T(8,128)S(1)}, f32[32,32]{1,0:T(8,128)S(1)}, u32[]{:S(2)}, u32[]{:S(2)}) collective-permute-start(f32[32,32]{1,0:T(8,128)S(1)} %convolution_subtract_fusion.20), channel_id=1, source_target_pairs={{0,8},{8,16},{16,24},{1,9},{9,17},{17,25},{2,10},{10,18},{18,26},{... | collective-permute-start | bytes 12296 | tf_op jit(solution)/shard_map/ppermute | solution.py:17
  844.7 48.2 %collective-permute-start.1 = (f32[32,4096]{1,0:T(8,128)S(1)}, f32[32,4096]{1,0:T(8,128)}, u32[]{:S(2)}, u32[]{:S(2)}) collective-permute-start(f32[32,4096]{1,0:T(8,128)S(1)} %convolution_subtract_fusion), channel_id=1, source_target_pairs={{0,8},{8,16},{16,24},{1,9},{9,17},{17,25},{2,10},{10,18},{18,26},{... | collective-permute-start | bytes 1572872 | tf_op jit(solution)/shard_map/ppermute | solution.py:17
  864.3 8.8 copy-start
  (14 other events, 64.8 us)
Sparse Core Ops, SparseCore 0:
  22.0 56.6 all-reduce.3
  225.6 83.1 all-gather.4
  333.6 56.0 all-reduce.5
  391.1 83.1 all-gather.8
  548.4 83.1 all-gather.10
  633.0 80.5 all-gather.6
where the time goes:
time: 926 us; the launch traced here: 911 us
  waiting for transfers between devices  349 us (38%)
  other arithmetic  271 us (29%)
  matrix products  189 us (20%)
  local copies, waits for them, and re-layouts  68.4 us (7%)
  between operations  20.9 us (2%)
  starting transfers between devices  11.2 us (1%)
    another operation x29, other arithmetic, local(): factor = jnp.linalg.cholesky(pivot_blk)  158 us
    ppermute x3, waiting for transfers between devices, shifted(): lax.ppermute(value, axis, [(source, source + steps) for source in range(l...  151 us
    dot_general x12, matrix products, outer_rows(): lax.dot_general(left_rows, right_rows, (((1,), (1,)), ((), ())), precisio...  134 us
    psum x2, waiting for transfers between devices, broadcast(): return lax.psum(block, axis)  82.8 us
    another operation x5, other arithmetic, solve_rows(): return jax.scipy.linalg.solve_triangular(factor, block.T, lower=True).T  79.9 us
    all_gather x2, waiting for transfers between devices, local(): factor_whole_a = lax.all_gather(factor_local_a, 'tile', axis=0, tiled=True)  76 us
    another operation x42, matrix products, solve_rows(): return jax.scipy.linalg.solve_triangular(factor, block.T, lower=True).T  47 us
    all_gather x2, waiting for transfers between devices, local(): factor_whole_c = lax.all_gather(factor_local_c, 'tile', axis=0, tiled=True)  39.2 us
  transfers between devices with their start and end apart: 9, of which 5 were waited for; matrix products, arithmetic and copies ran while one was open for 36% of the time, Pallas kernels for 0%

commit v1 on v0

v1 whole, which is shorter than its diff:
```python
import jax
import jax.numpy as jnp
from jax import lax
from jax.experimental import pallas as pl
from jax.experimental.pallas import tpu as pltpu
from jax.sharding import PartitionSpec as P

BLK = 128
precise = lax.Precision.HIGHEST


def dot_nt(a, b):
    return lax.dot_general(a, b, (((1,), (1,)), ((), ())), precision=precise, preferred_element_type=jnp.float32)


def dot_nn(a, b):
    return lax.dot_general(a, b, (((1,), (0,)), ((), ())), precision=precise, preferred_element_type=jnp.float32)


def spread_lane(tile, lane):
    return jnp.broadcast_to(tile[:, lane:lane + 1], (8, BLK))


def spread_row(tile, row):
    return jnp.broadcast_to(tile[row:row + 1, :], (8, BLK))


def diag_inverse(block_ref, inverse_ref):
    groups = BLK // 8
    sub = lax.broadcasted_iota(jnp.int32, (8, BLK), 0)
    lane = lax.broadcasted_iota(jnp.int32, (8, BLK), 1)
    left = [block_ref[8 * g:8 * g + 8, :] for g in range(groups)]
    right = [jnp.where(lane == sub + 8 * g, 1.0, 0.0).astype(jnp.float32) for g in range(groups)]
    for g in range(groups):
        rows, unit = left[g], right[g]
        cols = [spread_lane(rows, 8 * g + c) for c in range(8)]
        scale = jnp.zeros((8, BLK), jnp.float32)
        kept = []
        for k in range(8):
            pivot = spread_row(cols[k], k)
            inv = 1.0 / pivot
            scale = jnp.where(sub == k, lax.rsqrt(pivot), scale)
            row_l, row_r = spread_row(rows, k), spread_row(unit, k)
            heads = {c: spread_row(cols[c], k) for c in range(k + 1, 8)}
            kept.append((inv, row_l, row_r, heads))
            if k < 7:
                f = jnp.where(sub > k, cols[k] * inv, 0.0)
                for c in range(k + 1, 8):
                    cols[c] = cols[c] - f * heads[c]
                rows = rows - f * row_l
                unit = unit - f * row_r
        inverse_ref[8 * g:8 * g + 8, :] = unit * scale
        for r in range(g + 1, groups):
            fac = [spread_lane(left[r], 8 * g + c) for c in range(8)]
            lo, ro = left[r], right[r]
            for k in range(8):
                inv, row_l, row_r, heads = kept[k]
                f = fac[k] * inv
                for c in range(k + 1, 8):
                    fac[c] = fac[c] - f * heads[c]
                lo = lo - f * row_l
                ro = ro - f * row_r
            left[r], right[r] = lo, ro


def chain_kernel(k_ref, out_ref, l_ref, s_ref, g_ref, d_ref, m_ref):
    n = k_ref.shape[0]
    nb = n // BLK
    out_ref[...] = jnp.zeros((n, n), jnp.float32)

    def step(k, carry):
        for i in range(nb):
            @pl.when(k == i)
            def _(i=i):
                at, to = i * BLK, (i + 1) * BLK
                s = k_ref[at:, at:to]
                if i:
                    s = s - dot_nt(l_ref[at:, :at], l_ref[at:to, :at])
                    g_ref[:, :at] = dot_nn(l_ref[at:to, :at], out_ref[:at, :at])
                s_ref[at:, :] = s
                d_ref[...] = s[:BLK]

        diag_inverse(d_ref, m_ref)
        for i in range(nb):
            @pl.when(k == i)
            def _(i=i):
                at, to = i * BLK, (i + 1) * BLK
                m = m_ref[...]
                if i < nb - 1:
                    l_ref[to:, at:to] = dot_nt(s_ref[to:, :], m)
                out_ref[at:to, at:to] = m
                if i:
                    out_ref[at:to, :at] = -dot_nn(m, g_ref[:, :at])
        return carry

    lax.fori_loop(0, nb, step, 0)


def chain(k):
    n = k.shape[0]
    return pl.pallas_call(
        chain_kernel,
        out_shape=jax.ShapeDtypeStruct((n, n), jnp.float32),
        in_specs=[pl.BlockSpec(memory_space=pltpu.VMEM)],
        out_specs=pl.BlockSpec(memory_space=pltpu.VMEM),
        scratch_shapes=[pltpu.VMEM((n, n), jnp.float32), pltpu.VMEM((n, BLK), jnp.float32),
                        pltpu.VMEM((BLK, n), jnp.float32), pltpu.VMEM((BLK, BLK), jnp.float32),
                        pltpu.VMEM((BLK, BLK), jnp.float32)],
        compiler_params=pltpu.CompilerParams(vmem_limit_bytes=40 << 20),
        cost_estimate=pl.CostEstimate(flops=60_000_000_000, bytes_accessed=8 << 20, transcendentals=0),
    )(k)


def nt(left, right):
    return lax.dot_general(left, right, (((1,), (1,)), ((), ())), precision=lax.Precision.HIGH, preferred_element_type=jnp.float32)


def nn(left, right):
    return lax.dot_general(left, right, (((1,), (0,)), ((), ())), precision=lax.Precision.HIGH, preferred_element_type=jnp.float32)


def handed(value):
    count = lax.axis_size("tm")
    return lax.ppermute(value, "tm", [(t, t + 1) for t in range(count - 1)])


def gather_rows(own):
    return lax.all_gather(own, "tile", axis=0, tiled=True)


def local(diag_blocks, coupling, next_diag, arrow_now, arrow_next, arrow_tip):
    rows, cols = diag_blocks.shape
    pivots = cols // 4
    arrows = arrow_now.shape[0]
    panel_a, panel_c, panel_r = diag_blocks[:, :pivots], coupling[:, :pivots], arrow_now[:, :pivots]
    cut = rows * 3 // 4
    past_c = handed(panel_c)
    past_d = [handed(next_diag[:cut]), handed(next_diag[cut:])]
    past_b = handed(arrow_next)
    all_a = gather_rows(panel_a)
    inverse = chain(all_a[:pivots])
    solved = nt(jnp.concatenate([panel_a, panel_c, panel_r]), inverse)
    weight = nn(solved, inverse)
    past_w = handed(weight[rows:])
    past_tip = handed(arrow_tip - nt(solved[2 * rows:], solved[2 * rows:]))
    rest = nt(weight, all_a[pivots:])
    row_ids = lax.axis_index("tile") * rows + lax.iota(jnp.int32, rows)
    keep = lax.iota(jnp.int32, cols)[None, :] <= row_ids[:, None]
    factor = jnp.concatenate([solved[:rows], diag_blocks[:, pivots:] - rest[:rows]], axis=1)
    factor = jnp.where(keep, factor, 0.0)
    coupled = jnp.concatenate([solved[rows:2 * rows], coupling[:, pivots:] - rest[rows:2 * rows]], axis=1)
    arrow = jnp.concatenate([solved[2 * rows:], arrow_now[:, pivots:] - rest[2 * rows:]], axis=1)
    all_c = gather_rows(past_c)
    past_d = jnp.concatenate([past_d[0] - nt(past_w[:cut], all_c), past_d[1] - nt(past_w[cut:rows], all_c)])
    past_b = past_b - nt(past_w[rows:], all_c)
    return (factor, coupled, arrow, past_d, past_b, past_tip)


def solution(mesh):
    split, whole = P(("tm", "tile"), None), P("tm", None)
    return jax.shard_map(
        local,
        mesh=mesh,
        in_specs=(split, split, split, whole, whole, whole),
        out_specs=(split, split, whole, split, whole, whole),
        check_vma=False,
    )
```

time: 926 us -> 375 us (0.40); the launches traced: 911 us -> 369 us
  other arithmetic: 271 us -> 23.7 us
  waiting for transfers between devices: 349 us -> 156 us
  matrix products: 189 us -> 82.9 us
  Pallas kernels: 0 us -> 46.9 us
  local copies, waits for them, and re-layouts: 68.4 us -> 27.7 us
    another operation x38 -> x0, other arithmetic: 242 us -> none  [the longest x29 158 us: local(): factor = jnp.linalg.cholesky(pivot_blk)]
    psum x2 -> x0, waiting for transfers between devices: 82.8 us -> none  [broadcast(): return lax.psum(block, axis)]
    ppermute x3 -> x6, waiting for transfers between devices: 151 us -> 71.3 us  [handed(): return lax.ppermute(value, 'tm', [(t, t + 1) for t in range(count - 1)])]
    another operation x54 -> x0, matrix products: 55.7 us -> none  [the longest x42 47 us: solve_rows(): return jax.scipy.linalg.solve_triangular(factor, block.T, lower=True).T]
    dot_general x12 -> x7, matrix products: 134 us -> 82.9 us  [the longest x6 75.6 us: nt(): lax.dot_general(left, right, (((1,), (1,)), ((), ())), precision=lax.Prec...]
    pallas_call x0 -> x1, Pallas kernels: none -> 46.9 us  [chain(): pl.pallas_call(chain_kernel, out_shape=jax.ShapeDtypeStruct((n, n), jnp.f...]
    all_gather x4 -> x2, waiting for transfers between devices: 115 us -> 84.2 us  [gather_rows(): return lax.all_gather(own, 'tile', axis=0, tiled=True)]
    another operation x51 -> x0, local copies, waits for them, and re-layouts: 28.5 us -> none  [the longest x39 27.9 us: solve_rows(): return jax.scipy.linalg.solve_triangular(factor, block.T, lower=True).T]
  transfers between devices with their start and end apart: 9 -> 8, of which waited for: 5 -> 4; matrix products, arithmetic and copies ran while one was open for 36% -> 30% of each run, Pallas kernels for 0% -> 13%
where the time goes in v1:
time: 375 us; the launch traced here: 369 us
  waiting for transfers between devices  156 us (42%)
  matrix products  82.9 us (22%)
  Pallas kernels  46.9 us (13%)
  local copies, waits for them, and re-layouts  27.7 us (7%)
  other arithmetic  23.7 us (6%)
  starting transfers between devices  17.7 us (5%)
  between operations  14.6 us (4%)
    all_gather x2, waiting for transfers between devices, gather_rows(): return lax.all_gather(own, 'tile', axis=0, tiled=True)  84.2 us
    dot_general x6, matrix products, nt(): lax.dot_general(left, right, (((1,), (1,)), ((), ())), precision=lax.Prec...  75.6 us
    ppermute x6, waiting for transfers between devices, handed(): return lax.ppermute(value, 'tm', [(t, t + 1) for t in range(count - 1)])  71.3 us
    pallas_call x1, Pallas kernels, chain(): pl.pallas_call(chain_kernel, out_shape=jax.ShapeDtypeStruct((n, n), jnp.f...  46.9 us
    ppermute x6, starting transfers between devices, handed(): return lax.ppermute(value, 'tm', [(t, t + 1) for t in range(count - 1)])  17.6 us
    sub x1, other arithmetic, local(): coupling[:, pivots:] - rest[rows:2 * rows]  9.65 us
    slice x2, local copies, waits for them, and re-layouts, local(): past_d = [handed(next_diag[:cut]), handed(next_diag[cut:])]  9.38 us
    unnamed x17, local copies, waits for them, and re-layouts  8 us
  transfers between devices with their start and end apart: 8, of which 4 were waited for; matrix products, arithmetic and copies ran while one was open for 30% of the time, Pallas kernels for 13%

profile of v1, /device:TPU:19, one launch (start us, length us, event | category | flops | bytes accessed | tf_op | source)
XLA Modules:
  0.0 369.0 jit_solution(4121275694827196222)
XLA Ops:
  7.2 3.2 slice.62
  13.5 3.1 collective-permute-start.2
  16.6 45.4 %collective-permute-done.2 = f32[512,1024]{1,0:T(8,128)S(1)} collective-permute-done((f32[512,1024]{1,0:T(8,128)S(1)}, f32[512,1024]{1,0:T(8,128)S(1)}, u32[]{:S(2)}, u32[]{:S(2)}) %collective-permute-start.2) | collective-permute-done | bytes 2097184 | tf_op jit(solution)/shard_map/ppermute | solution.py:124
  63.4 3.1 slice.79
  66.5 4.0 %collective-permute-start.3 = (f32[128,4096]{1,0:T(8,128)}, f32[128,4096]{1,0:T(8,128)}, u32[]{:S(2)}, u32[]{:S(2)}) collective-permute-start(f32[128,4096]{1,0:T(8,128)} %slice.79), channel_id=1, source_target_pairs={{0,8},{8,16},{16,24},{1,9},{9,17},{17,25},{2,10},{10,18},{18,26},{... | collective-permute-start | bytes 6291464 | tf_op jit(solution)/shard_map/ppermute | solution.py:124
  70.5 6.2 %slice.76 = f32[384,4096]{1,0:T(8,128)} slice(f32[512,4096]{1,0:T(8,128)} %param.8), slice={[0:384], [0:4096]} | slice | bytes 12582912 | tf_op jit(solution)/shard_map/slice | solution.py:138
  81.0 80.4 %all-gather.3.cloned.1.call-done = f32[4096,1024]{1,0:T(8,128)} async-done(((f32[512,1024]{1,0:T(8,128)}), f32[4096,1024]{1,0:T(8,128)}) %all-gather.3.cloned.1.call-update) | async-done | bytes 16777232 | tf_op jit(solution)/shard_map/all_gather | solution.py:128
  161.4 2.8 slice.82.k_ref
  164.2 46.9 %shard_map.109 = f32[1024,1024]{1,0:T(8,128)S(1)} custom-call(f32[1024,1024]{1,0:T(8,128)S(1)} %slice.82.k_ref), custom_call_target="tpu_custom_call" | custom-call | flops 60000002048 | bytes 8388608 | tf_op jit(solution)/shard_map/pallas_call | solution.py:101
  211.1 7.2 %fusion.2 = f32[1056,1024]{1,0:T(8,128)S(1)} fusion(f32[1024,1024]{1,0:T(8,128)S(1)} %shard_map.109, f32[32,1024]{1,0:T(8,128)S(1)} %slice-done.1, f32[512,1024]{1,0:T(8,128)S(1)} %copy-done.5, f32[512,1024]{1,0:T(8,128)S(1)} %copy-done.1), kind=kOutput, calls=%fused_computation.11 | convolution fusion | flops 6645940224 | bytes 12845056 | tf_op jit(solution)/shard_map/dot_general | solution.py:115
  218.3 7.3 %fusion.14 = f32[1056,1024]{1,0:T(8,128)S(1)} fusion(f32[1056,1024]{1,0:T(8,128)S(1)} %fusion.2, f32[1024,1024]{1,0:T(8,128)S(1)} %shard_map.109), kind=kOutput, calls=%fused_computation.27 | convolution fusion | flops 6643777536 | bytes 12845056 | tf_op jit(solution)/shard_map/dot_general | solution.py:119
  225.8 3.2 collective-permute-start.1
  229.0 23.7 %fusion = f32[1056,3072]{1,0:T(8,128)S(1)} fusion(f32[1056,1024]{1,0:T(8,128)S(1)} %fusion.14, f32[4096,1024]{1,0:T(8,128)} %all-gather.3.cloned.1.call-done), kind=kOutput, calls=%fused_computation | convolution fusion | flops 19931332608 | bytes 29884416 | tf_op jit(solution)/shard_map/dot_general | solution.py:115
  252.8 4.7 %copy-done = f32[1056,3072]{1,0:T(8,128)} copy-done((f32[1056,3072]{1,0:T(8,128)}, f32[1056,3072]{1,0:T(8,128)S(1)}, u32[]{:S(2)}) %copy-start) | copy-done | bytes 12976152
  258.2 9.6 %slice_subtract_fusion = (f32[512,3072]{1,0:T(8,128)S(1)}, f32[512,3072]{1,0:T(8,128)S(1)}) fusion(f32[1056,3072]{1,0:T(8,128)} %copy-done, f32[512,4096]{1,0:T(8,128)} %param.7, f32[512,4096]{1,0:T(8,128)} %param.6), kind=kLoop, calls=%fused_computation.6 | loop fusion | flops 3145728 | bytes 37748736 | tf_op jit(solution)/shard_map/sub | solution.py:151
  268.1 3.1 collective-permute-start.5
  271.2 2.5 fusion.13
  273.8 7.1 %maximum_select_fusion = (f32[512,4096]{1,0:T(8,128)}, f32[512,4096]{1,0:T(8,128)}) fusion(f32[512,3072]{1,0:T(8,128)S(1)} %get-tuple-element.7, f32[512,1024]{1,0:T(8,128)S(1)} %get-tuple-element.9, s32[512]{0:T(512)S(1)} %iota_add_fusion, f32[512,3072]{1,0:T(8,128)S(1)} %get-tuple-element.6, f32[512,1024]{1,0:T(8,128)S(1)} %get-tuple-element.8), kind=kLoop, calls=%fused_computation.2 | loop fusion | flops 8388608 | bytes 33556480 | tf_op jit(solution)/shard_map/jit(_where)/select_n | solution.py:150
  282.6 25.9 %collective-permute-done.5 = f32[32,32]{1,0:T(8,128)S(1)} collective-permute-done((f32[32,32]{1,0:T(8,128)S(1)}, f32[32,32]{1,0:T(8,128)S(1)}, u32[]{:S(2)}, u32[]{:S(2)}) %collective-permute-start.5) | collective-permute-done | bytes 4128 | tf_op jit(solution)/shard_map/ppermute | solution.py:124
  308.6 3.8 %all-gather.5.cloned.1.call-done = f32[4096,1024]{1,0:T(8,128)} async-done(((f32[512,1024]{1,0:T(8,128)}), f32[4096,1024]{1,0:T(8,128)}) %all-gather.5.cloned.1.call-update) | async-done | bytes 16777232 | tf_op jit(solution)/shard_map/all_gather | solution.py:128
  312.4 14.9 %convolution_subtract_fusion.1 = f32[128,4096]{1,0:T(8,128)S(1)} fusion(f32[128,4096]{1,0:T(8,128)} %collective-permute-done.3, f32[4096,1024]{1,0:T(8,128)} %all-gather.5.cloned.1.call-done, f32[544,1024]{1,0:T(8,128)} %collective-permute-done.1), kind=kOutput, calls=%fused_computation.9 | convolution fusion | flops 3221749760 | bytes 21495808 | tf_op jit(solution)/shard_map/dot_general | solution.py:115
  327.3 15.7 %convolution_subtract_fusion = f32[384,4096]{1,0:T(8,128)S(1)} fusion(f32[384,4096]{1,0:T(8,128)} %collective-permute-done, f32[4096,1024]{1,0:T(8,128)} %all-gather.5.cloned.1.call-done, f32[544,1024]{1,0:T(8,128)} %collective-permute-done.1), kind=kOutput, calls=%fused_computation.8 | convolution fusion | flops 9665249280 | bytes 30932992 | tf_op jit(solution)/shard_map/dot_general | solution.py:115
  343.0 4.4 %pad_maximum_fusion.1 = f32[512,4096]{1,0:T(8,128)} fusion(f32[128,4096]{1,0:T(8,128)S(1)} %convolution_subtract_fusion.1, f32[384,4096]{1,0:T(8,128)S(1)} %convolution_subtract_fusion), kind=kLoop, calls=%fused_computation.4 | loop fusion | flops 2097152 | bytes 16777216 | tf_op jit(solution)/shard_map/concatenate | solution.py:154
  347.4 13.9 %convolution_subtract_fusion.2 = f32[32,4096]{1,0:T(8,128)} fusion(f32[32,4096]{1,0:T(8,128)} %collective-permute-done.4, f32[4096,1024]{1,0:T(8,128)} %all-gather.5.cloned.1.call-done, f32[544,1024]{1,0:T(8,128)} %collective-permute-done.1), kind=kOutput, calls=%fused_computation.10 | convolution fusion | flops 805437440 | bytes 17956864 | tf_op jit(solution)/shard_map/dot_general | solution.py:115
  (36 shorter events, 12.3 us)
Async XLA Ops:
  7.2 154.2 %all-gather.3.cloned.1.call-start = ((), (), s32[]{:S(2)}) async-start(), calls=%async_computation | async-start | bytes 18874368 | tf_op jit(solution)/shard_map/all_gather | solution.py:128
  10.4 302.0 %all-gather.5.cloned.1.call-start = ((), (), s32[]{:S(2)}) async-start(), calls=%async_computation.1 | async-start | bytes 18874368 | tf_op jit(solution)/shard_map/all_gather | solution.py:128
  12.2 1.3 copy-start.4
  13.5 48.5 %collective-permute-start.2 = (f32[512,1024]{1,0:T(8,128)S(1)}, f32[512,1024]{1,0:T(8,128)S(1)}, u32[]{:S(2)}, u32[]{:S(2)}) collective-permute-start(f32[512,1024]{1,0:T(8,128)S(1)} %slice.63), channel_id=1, source_target_pairs={{0,8},{8,16},{16,24},{1,9},{9,17},{17,25},{2,10},{10,18},{18,26},{... | collective-permute-start | bytes 6291464 | tf_op jit(solution)/shard_map/ppermute | solution.py:124
  62.0 1.4 copy-start.3
  66.5 242.0 %collective-permute-start.3 = (f32[128,4096]{1,0:T(8,128)}, f32[128,4096]{1,0:T(8,128)}, u32[]{:S(2)}, u32[]{:S(2)}) collective-permute-start(f32[128,4096]{1,0:T(8,128)} %slice.79), channel_id=1, source_target_pairs={{0,8},{8,16},{16,24},{1,9},{9,17},{17,25},{2,10},{10,18},{18,26},{... | collective-permute-start | bytes 6291464 | tf_op jit(solution)/shard_map/ppermute | solution.py:124
  76.8 250.5 %collective-permute-start = (f32[384,4096]{1,0:T(8,128)}, f32[384,4096]{1,0:T(8,128)}, u32[]{:S(2)}, u32[]{:S(2)}) collective-permute-start(f32[384,4096]{1,0:T(8,128)} %slice.76), channel_id=1, source_target_pairs={{0,8},{8,16},{16,24},{1,9},{9,17},{17,25},{2,10},{10,18},{18,26},{... | collective-permute-start | bytes 18874376 | tf_op jit(solution)/shard_map/ppermute | solution.py:124
  79.0 268.4 %collective-permute-start.4 = (f32[32,4096]{1,0:T(8,128)}, f32[32,4096]{1,0:T(8,128)}, u32[]{:S(2)}, u32[]{:S(2)}) collective-permute-start(f32[32,4096]{1,0:T(8,128)} %param.10), channel_id=1, source_target_pairs={{0,8},{8,16},{16,24},{1,9},{9,17},{17,25},{2,10},{10,18},{18,26},{... | collective-permute-start | bytes 1572872 | tf_op jit(solution)/shard_map/ppermute | solution.py:124
  164.1 47.0 %copy-start.1 = (f32[512,1024]{1,0:T(8,128)S(1)}, f32[512,1024]{1,0:T(8,128)}, u32[]{:S(2)}) copy-start(f32[512,1024]{1,0:T(8,128)} %slice.62) | copy-start | bytes 6291460
  164.1 47.0 %copy-start.5 = (f32[512,1024]{1,0:T(8,128)S(1)}, f32[512,1024]{1,0:T(8,128)}, u32[]{:S(2)}) copy-start(f32[512,1024]{1,0:T(8,128)} %copy-done.4) | copy-start | bytes 6291460
  164.2 47.0 %slice-start.1 = ((f32[32,4096]{1,0:T(8,128)}), f32[32,1024]{1,0:T(8,128)S(1)}, s32[]{:S(2)}) async-start(f32[32,4096]{1,0:T(8,128)} %param.9), calls=%async_computation.3 | async-start | bytes 262144 | tf_op jit(solution)/shard_map/slice | solution.py:135
  218.3 49.8 %copy-start.2 = (f32[1056,1024]{1,0:T(8,128)}, f32[1056,1024]{1,0:T(8,128)S(1)}, u32[]{:S(2)}) copy-start(f32[1056,1024]{1,0:T(8,128)S(1)} %fusion.2) | copy-start | bytes 12976132
  225.8 31.7 %copy-start.6 = (f32[32,4096]{1,0:T(8,128)S(1)}, f32[32,4096]{1,0:T(8,128)}, u32[]{:S(2)}) copy-start(f32[32,4096]{1,0:T(8,128)} %param.9) | copy-start | bytes 1572868
  225.8 86.6 %collective-permute-start.1 = (f32[544,1024]{1,0:T(8,128)S(1)}, f32[544,1024]{1,0:T(8,128)}, u32[]{:S(2)}, u32[]{:S(2)}) collective-permute-start(f32[544,1024]{1,0:T(8,128)S(1)} %slice.90), channel_id=1, source_target_pairs={{0,8},{8,16},{16,24},{1,9},{9,17},{17,25},{2,10},{10,18},{18,26},{... | collective-permute-start | bytes 6684680 | tf_op jit(solution)/shard_map/ppermute | solution.py:124
  252.8 4.7 %copy-start = (f32[1056,3072]{1,0:T(8,128)}, f32[1056,3072]{1,0:T(8,128)S(1)}, u32[]{:S(2)}) copy-start(f32[1056,3072]{1,0:T(8,128)S(1)} %fusion) | copy-start | bytes 38928388
  258.2 9.7 %copy-start.7 = (f32[32,32]{1,0:T(8,128)S(1)}, f32[32,32]{1,0:T(8,128)}, u32[]{:S(2)}) copy-start(f32[32,32]{1,0:T(8,128)} %param.11) | copy-start | bytes 12292
  268.1 40.4 %collective-permute-start.5 = (f32[32,32]{1,0:T(8,128)S(1)}, f32[32,32]{1,0:T(8,128)S(1)}, u32[]{:S(2)}, u32[]{:S(2)}) collective-permute-start(f32[32,32]{1,0:T(8,128)S(1)} %convolution_subtract_fusion.3), channel_id=1, source_target_pairs={{0,8},{8,16},{16,24},{1,9},{9,17},{17,25},{2,10},{10,18},{18,26},{... | collective-permute-start | bytes 12296 | tf_op jit(solution)/shard_map/ppermute | solution.py:124
  273.7 7.1 %slice-start = ((f32[1056,1024]{1,0:T(8,128)}), f32[32,1024]{1,0:T(8,128)S(1)}, s32[]{:S(2)}) async-start(f32[1056,1024]{1,0:T(8,128)} %copy-done.2), calls=%async_computation.2 | async-start | bytes 262144 | tf_op jit(solution)/shard_map/slice | solution.py:152
Sparse Core Ops, SparseCore 0:
  10.5 150.8 all-gather.2
  163.0 149.3 all-gather.4

commit v2 on v1

--- a/solution.py
+++ b/solution.py
@@ -1,3 +1,5 @@
+import functools
+
 import jax
 import jax.numpy as jnp
 from jax import lax
@@ -107,8 +109,170 @@
                         pltpu.VMEM((BLK, n), jnp.float32), pltpu.VMEM((BLK, BLK), jnp.float32),
                         pltpu.VMEM((BLK, BLK), jnp.float32)],
         compiler_params=pltpu.CompilerParams(vmem_limit_bytes=40 << 20),
-        cost_estimate=pl.CostEstimate(flops=60_000_000_000, bytes_accessed=8 << 20, transcendentals=0),
+        cost_estimate=pl.CostEstimate(flops=1_000_000, bytes_accessed=1 << 16, transcendentals=0),
     )(k)
+
+
+def chain_picked_kernel(at_ref, *refs):
+    pairs, (out_ref, k_ref, l_ref, s_ref, g_ref, d_ref, m_ref) = refs[:6], refs[6:]
+    rows = k_ref.shape[0] // 2
+    for which in range(3):
+        for core in range(2):
+            @pl.when((at_ref[0] == which) & (at_ref[1] == core))
+            def _(which=which, core=core):
+                pltpu.sync_copy(pairs[2 * which], k_ref.at[core * rows:(core + 1) * rows])
+                pltpu.sync_copy(pairs[2 * which + 1], k_ref.at[(1 - core) * rows:(2 - core) * rows])
+    chain_kernel(k_ref, out_ref, l_ref, s_ref, g_ref, d_ref, m_ref)
+
+
+def chain_picked(at, pairs):
+    n = 2 * pairs[0].shape[0]
+    return pl.pallas_call(
+        chain_picked_kernel,
+        out_shape=jax.ShapeDtypeStruct((n, n), jnp.float32),
+        grid_spec=pltpu.PrefetchScalarGridSpec(
+            num_scalar_prefetch=1,
+            grid=(1,),
+            in_specs=[pl.BlockSpec(memory_space=pl.ANY)] * 6,
+            out_specs=pl.BlockSpec((n, n), lambda i, at: (0, 0)),
+            scratch_shapes=[pltpu.VMEM((n, n), jnp.float32), pltpu.VMEM((n, n), jnp.float32), pltpu.VMEM((n, BLK), jnp.float32),
+                            pltpu.VMEM((BLK, n), jnp.float32), pltpu.VMEM((BLK, BLK), jnp.float32),
+                            pltpu.VMEM((BLK, BLK), jnp.float32)],
+        ),
+        compiler_params=pltpu.CompilerParams(vmem_limit_bytes=40 << 20),
+        cost_estimate=pl.CostEstimate(flops=1_000_000, bytes_accessed=1 << 16, transcendentals=0),
+    )(at, *pairs)
+
+
+def halves(x):
+    high = x.astype(jnp.bfloat16)
+    return high, (x - high.astype(jnp.float32)).astype(jnp.bfloat16)
+
+
+def product(weights, other):
+    (high, low), (other_high, other_low) = weights, other
+    dims = (((1,), (1,)), ((), ()))
+    total = lax.dot_general(high, other_high, dims, preferred_element_type=jnp.float32)
+    total += lax.dot_general(high, other_low, dims, preferred_element_type=jnp.float32)
+    return total + lax.dot_general(low, other_high, dims, preferred_element_type=jnp.float32)
+
+
+LIGHT = pl.CostEstimate(flops=1_000_000, bytes_accessed=1 << 16, transcendentals=0)
+
+
+def fetch(step, sources, buffer_ref, sems):
+    for i in range(len(sources)):
+        @pl.when(step == i)
+        def _(i=i):
+            copies = [pltpu.make_async_copy(sources[j], buffer_ref.at[j % 2], sems.at[j % 2])
+                      for j in (i, i + 1) if j < len(sources)]
+            if i == 0:
+                copies[0].start()
+            if len(copies) > 1:
+                copies[1].start()
+            copies[0].wait()
+
+
+def panel_update_kernel(count, at_ref, high_ref, low_ref, solved_ref, a_ref, c_ref, r_ref, *rest):
+    a_out, c_out, r_out, buffer_ref, sems = rest[-5:]
+    step = pl.program_id(0)
+    rows = a_ref.shape[0]
+    fetch(step, rest[:count], buffer_ref, sems)
+    block = at_ref[step]
+    keep = (block * rows + lax.broadcasted_iota(jnp.int32, (rows, rows), 1)
+            <= at_ref[count] + lax.broadcasted_iota(jnp.int32, (rows, rows), 0))
+    solved = block * rows < high_ref.shape[1]
+
+    @pl.when(solved)
+    def _():
+        a_out[...] = jnp.where(keep, solved_ref[:rows], 0.0)
+        c_out[...] = solved_ref[rows:2 * rows]
+        r_out[...] = solved_ref[2 * rows:]
+
+    @pl.when(jnp.logical_not(solved))
+    def _():
+        x = halves(buffer_ref[step % 2])
+        a_out[...] = jnp.where(keep, a_ref[...] - product((high_ref[:rows], low_ref[:rows]), x), 0.0)
+        c_out[...] = c_ref[...] - product((high_ref[rows:2 * rows], low_ref[rows:2 * rows]), x)
+        r_out[...] = r_ref[...] - product((high_ref[2 * rows:], low_ref[2 * rows:]), x)
+
+
+def panel_update(at, weights, solved, bases, blocks, before):
+    rows, arrows, pivots = bases[0].shape[0], bases[2].shape[0], solved.shape[1]
+    last = pivots // rows - 1
+    count = len(blocks)
+    whole = pl.BlockSpec(memory_space=pl.ANY)
+    fixed = pl.BlockSpec((2 * rows + arrows, pivots), lambda i, at: (0, 0))
+    moving = [pl.BlockSpec((h, rows), lambda i, at: (0, at[i])) for h in (rows, rows, arrows)]
+    in_specs = [fixed] * 2 + [pl.BlockSpec((2 * rows + arrows, rows), lambda i, at: (0, jnp.minimum(at[i], last)))]
+    in_specs += moving + [whole] * count
+    args = [at, *weights, solved, *bases, *blocks]
+    aliases = {}
+    if before is not None:
+        aliases = {len(args) + i: i for i in range(3)}
+        in_specs += [whole] * 3
+        args += list(before)
+    return pl.pallas_call(
+        functools.partial(panel_update_kernel, count),
+        out_shape=[jax.ShapeDtypeStruct(b.shape, b.dtype) for b in bases],
+        grid_spec=pltpu.PrefetchScalarGridSpec(
+            num_scalar_prefetch=1, grid=(count,), in_specs=in_specs,
+            out_specs=moving,
+            scratch_shapes=[pltpu.VMEM((2, rows, pivots), jnp.float32), pltpu.SemaphoreType.DMA((2,))]),
+        input_output_aliases=aliases,
+        compiler_params=pltpu.CompilerParams(vmem_limit_bytes=48 << 20),
+        cost_estimate=LIGHT,
+    )(*args)
+
+
+def schur_update_kernel(count, parts, arrow, at_ref, high_ref, low_ref, *rest):
+    bases, sources, (*outs, buffer_ref, sems) = rest[:parts], rest[parts:parts + count], rest[-2 - (2 if arrow else 1):]
+    step = pl.program_id(0)
+    height, rows = outs[0].shape
+    fetch(step, sources, buffer_ref, sems)
+    x_ref = buffer_ref.at[step % 2]
+    x = halves(x_ref[:rows])
+    total = product((high_ref[:height], low_ref[:height]), x)
+    start = 0
+    for base in bases:
+        end = start + base.shape[0]
+        outs[0][start:end] = base[...] - total[start:end]
+        start = end
+    if arrow:
+        base = jnp.concatenate([x_ref[rows:, :rows], x_ref[rows:, rows:2 * rows]], axis=0)
+        outs[1][...] = base - product((high_ref[rows:], low_ref[rows:]), x)
+
+
+def schur_update(at, weights, bases, blocks, before, row_at=0, arrow=True):
+    rows, pivots = blocks[0].shape[0] - 16, blocks[0].shape[1]
+    arrows, cols = weights[0].shape[0] - rows, bases[0].shape[1]
+    height = sum(base.shape[0] for base in bases)
+    count = len(blocks)
+    whole = pl.BlockSpec(memory_space=pl.ANY)
+    fixed = pl.BlockSpec((rows + arrows if arrow else height, pivots), lambda i, at: (row_at, 0))
+    in_specs = [fixed] * 2 + [pl.BlockSpec((base.shape[0], rows), lambda i, at: (0, at[i])) for base in bases]
+    in_specs += [whole] * count
+    args = [at, *weights, *bases, *blocks]
+    out_shape = [jax.ShapeDtypeStruct((rows, cols), jnp.float32)]
+    out_specs = [pl.BlockSpec((height, rows), lambda i, at: (row_at, at[i]))]
+    if arrow:
+        out_shape.append(jax.ShapeDtypeStruct((arrows, cols), jnp.float32))
+        out_specs.append(pl.BlockSpec((arrows, rows), lambda i, at: (0, at[i])))
+    aliases = {}
+    if before is not None:
+        aliases = {len(args) + i: i for i in range(len(before))}
+        in_specs += [whole] * len(before)
+        args += list(before)
+    return pl.pallas_call(
+        functools.partial(schur_update_kernel, count, len(bases), arrow),
+        out_shape=out_shape,
+        grid_spec=pltpu.PrefetchScalarGridSpec(
+            num_scalar_prefetch=1, grid=(count,), in_specs=in_specs, out_specs=out_specs,
+            scratch_shapes=[pltpu.VMEM((2, rows + 16, pivots), jnp.float32), pltpu.SemaphoreType.DMA((2,))]),
+        input_output_aliases=aliases,
+        compiler_params=pltpu.CompilerParams(vmem_limit_bytes=48 << 20),
+        cost_estimate=LIGHT,
+    )(*args)
 
 
 def nt(left, right):
@@ -124,20 +288,100 @@
     return lax.ppermute(value, "tm", [(t, t + 1) for t in range(count - 1)])
 
 
-def gather_rows(own):
-    return lax.all_gather(own, "tile", axis=0, tiled=True)
+def after(value, *others):
+    return lax.optimization_barrier((value,) + others)[0]
+
+
+def stage(values, *others):
+    return lax.optimization_barrier(tuple(values) + others)[:len(values)]
+
+
+def hop(value, pairs):
+    return lax.ppermute(value, "tile", [(2 * a + c, 2 * b + c) for a, b in pairs for c in range(2)])
+
+
+def sibling(value):
+    return lax.ppermute(value, "tile", [(i, i ^ 1) for i in range(8)])
+
+
+def bf16_halves(x):
+    high = lax.reduce_precision(x, 8, 7)
+    return high.astype(jnp.bfloat16), (x - high).astype(jnp.bfloat16)
+
+
+def local_line(diag_blocks, coupling, next_diag, arrow_now, arrow_next, arrow_tip):
+    rows, cols = diag_blocks.shape
+    pivots = cols // 4
+    arrows = arrow_now.shape[0]
+    tile = lax.axis_index("tile")
+    chip, core = tile // 2, tile % 2
+    edge = (chip == 0) | (chip == 3)
+    panel_a, panel_c, panel_r = diag_blocks[:, :pivots], coupling[:, :pivots], arrow_now[:, :pivots]
+    part = lax.dynamic_slice(arrow_next, (0, tile * rows), (arrows, rows))
+    sent_c = jnp.concatenate([panel_c, jnp.concatenate([part[:16], part[16:]], axis=1)], axis=0)
+    first, second = [(0, 2), (3, 1), (2, 3), (1, 0)], [(0, 1), (2, 3), (3, 2), (1, 0)]
+    third, fourth = [(1, 3), (2, 0)], [(1, 2), (2, 1)]
+    near, end = rows // 4, rows * 3 // 4
+
+    e1 = hop(panel_a, first)
+    past_c = handed(sent_c)
+    o_own = sibling(panel_a)
+    e2 = hop(jnp.where(edge, panel_a, e1), second)
+    e4 = hop(after(panel_a, e1, past_c, o_own), fourth)
+    d1 = handed(after(next_diag[:near], past_c))
+    o_e1 = sibling(e1)
+    e3 = hop(after(panel_a, e2, e4), third)
+    f1 = hop(after(past_c, e2, e4), first)
+    d2 = handed(after(next_diag[near:end], e2, d1))
+    o_e2 = sibling(after(e2, d1, e4, o_own, o_e1))
+    pick = jnp.stack([jnp.where(chip == 0, 0, jnp.where(chip == 2, 1, 2)), core])
+    inverse = chain_picked(pick, [panel_a, o_own, e1, o_e1, e2, o_e2])
+    solved = nt(jnp.concatenate([panel_a, panel_c, panel_r]), inverse)
+    weight = nn(solved, inverse)
+
+    tip = arrow_tip - nt(solved[2 * rows:], solved[2 * rows:])
+    tip = jnp.pad(tip.reshape(1, -1), ((0, 7), (0, pivots - arrows * arrows)))
+    past_w = handed(jnp.concatenate([weight[rows:], tip]))
+    f1, e3, d2 = stage((f1, e3, d2), weight)
+    r3 = jnp.where(edge, e3, e4)
+    f2 = hop(jnp.where(edge, past_c, f1), second)
+    f4 = hop(after(past_c, f1), fourth)
+    o_f1, o_r3 = sibling(f1), sibling(r3)
+
+    def spots(*slots):
+        return [at for slot in slots for at in (2 * slot + core, 2 * slot + 1 - core)]
+
+    def table(entries):
+        return jnp.stack(entries).astype(jnp.int32)
+
+    early = spots(chip, (2 * chip + 1) % 5, 3 * (1 - chip % 2))
+    late = spots(2 - chip // 2)
+    split = bf16_halves(weight)
+    bases = (diag_blocks, coupling, arrow_now)
+    at = after(table(early + [tile * rows]), d2, f1, e3)
+    out = panel_update(at, split, solved, bases, [panel_a, o_own, e1, o_e1, e2, o_e2], None)
+    out = panel_update(table(late + [tile * rows]), split, solved, bases, [r3, o_r3], out)
+    past_w, f2, f4 = stage((past_w, f2, f4), out[2])
+    f3 = hop(after(past_c, f4, f2), third)
+    d3 = handed(after(next_diag[end:], past_w))
+    past_tip = past_w[rows + arrows, :arrows * arrows].reshape(arrows, arrows)
+    o_f2, o_c = sibling(f2), sibling(after(past_c, f2))
+    split = bf16_halves(past_w[:rows + arrows])
+    blocks = [past_c, o_c, f1, o_f1, f2, o_f2]
+    past_d, past_b = schur_update(table(early), split, [d1, d2], blocks, None)
+    d3, f3 = stage((d3, f3), past_b)
+    past_d, = schur_update(table(early), split, [d3], blocks, [past_d], rows // near - 1, False)
+    s3 = jnp.where(edge, f3, f4)
+    gone = schur_update(table(late), split, [d1, d2, d3], [s3, sibling(s3)], [past_d, past_b])
+    return (*out, *gone, past_tip)
 
 
 def local(diag_blocks, coupling, next_diag, arrow_now, arrow_next, arrow_tip):
     rows, cols = diag_blocks.shape
     pivots = cols // 4
-    arrows = arrow_now.shape[0]
     panel_a, panel_c, panel_r = diag_blocks[:, :pivots], coupling[:, :pivots], arrow_now[:, :pivots]
-    cut = rows * 3 // 4
-    past_c = handed(panel_c)
-    past_d = [handed(next_diag[:cut]), handed(next_diag[cut:])]
-    past_b = handed(arrow_next)
-    all_a = gather_rows(panel_a)
+    past_c, past_d, past_b = handed(panel_c), handed(next_diag), handed(arrow_next)
+    all_a = lax.all_gather(panel_a, "tile", axis=0, tiled=True)
     inverse = chain(all_a[:pivots])
     solved = nt(jnp.concatenate([panel_a, panel_c, panel_r]), inverse)
     weight = nn(solved, inverse)
@@ -150,8 +394,8 @@
     factor = jnp.where(keep, factor, 0.0)
     coupled = jnp.concatenate([solved[rows:2 * rows], coupling[:, pivots:] - rest[rows:2 * rows]], axis=1)
     arrow = jnp.concatenate([solved[2 * rows:], arrow_now[:, pivots:] - rest[2 * rows:]], axis=1)
-    all_c = gather_rows(past_c)
-    past_d = jnp.concatenate([past_d[0] - nt(past_w[:cut], all_c), past_d[1] - nt(past_w[cut:rows], all_c)])
+    all_c = lax.all_gather(past_c, "tile", axis=0, tiled=True)
+    past_d = past_d - nt(past_w[:rows], all_c)
     past_b = past_b - nt(past_w[rows:], all_c)
     return (factor, coupled, arrow, past_d, past_b, past_tip)
 
@@ -159,7 +403,7 @@
 def solution(mesh):
     split, whole = P(("tm", "tile"), None), P("tm", None)
     return jax.shard_map(
-        local,
+        local_line if mesh.shape["tile"] == 8 else local,
         mesh=mesh,
         in_specs=(split, split, split, whole, whole, whole),
         out_specs=(split, split, whole, split, whole, whole),

time: 375 us -> 356 us (0.949)
  Pallas kernels: 46.9 us -> 136 us
  matrix products: 82.9 us -> 22.2 us
  waiting for transfers between devices: 156 us -> 108 us
  starting transfers between devices: 17.7 us -> 41.9 us
  between operations: 14.6 us -> 1.1 us
  other arithmetic: 23.7 us -> 19.2 us
    pallas_call x1 -> x6, Pallas kernels: 46.9 us -> 136 us  [the longest x1 49.4 us: chain_picked(): pl.pallas_call(chain_picked_kernel, out_shape=jax.ShapeDtypeStruct((n, n)...]
    all_gather x2 -> x0, waiting for transfers between devices: 84.2 us -> none  [gather_rows(): return lax.all_gather(own, 'tile', axis=0, tiled=True)]
    dot_general x6 -> x2, matrix products: 75.6 us -> 10.6 us  [nt(): lax.dot_general(left, right, (((1,), (1,)), ((), ())), precision=lax.Prec...]
    ppermute x0 -> x16, waiting for transfers between devices: none -> 64.3 us  [the longest x8 64.1 us: hop(): lax.ppermute(value, 'tile', [(2 * a + c, 2 * b + c) for a, b in pairs for...]
    ppermute x6 -> x5, waiting for transfers between devices: 71.3 us -> 43.7 us  [handed(): return lax.ppermute(value, 'tm', [(t, t + 1) for t in range(count - 1)])]
    ppermute x0 -> x16, starting transfers between devices: none -> 26.2 us  [the longest x8 18.3 us: hop(): lax.ppermute(value, 'tile', [(2 * a + c, 2 * b + c) for a, b in pairs for...]
    sub x2 -> x0, other arithmetic: 10.4 us -> none  [the longest x1 9.65 us: local(): coupling[:, pivots:] - rest[rows:2 * rows]]
    select_n x1 -> x4, other arithmetic: 7.07 us -> 12 us  [the longest x1 3.64 us: local_line(): f2 = hop(jnp.where(edge, past_c, f1), second)]
  transfers between devices with their start and end apart: 8 -> 21, of which waited for: 4 -> 8; matrix products, arithmetic and copies ran while one was open for 30% -> 15% of each run, Pallas kernels for 13% -> 36%
where the time goes in v2:
time: 356 us; the launch traced here: 352 us
  Pallas kernels  136 us (38%)
  waiting for transfers between devices  108 us (30%)
  starting transfers between devices  41.9 us (12%)
  local copies, waits for them, and re-layouts  24 us (7%)
  matrix products  22.2 us (6%)
  other arithmetic  19.2 us (5%)
    ppermute x8, waiting for transfers between devices, hop(): lax.ppermute(value, 'tile', [(2 * a + c, 2 * b + c) for a, b in pairs for...  64.1 us
    pallas_call x1, Pallas kernels, chain_picked(): pl.pallas_call(chain_picked_kernel, out_shape=jax.ShapeDtypeStruct((n, n)...  49.4 us
    pallas_call x2, Pallas kernels, panel_update(): pl.pallas_call(functools.partial(panel_update_kernel, count), out_shape=[...  46.6 us
    ppermute x5, waiting for transfers between devices, handed(): return lax.ppermute(value, 'tm', [(t, t + 1) for t in range(count - 1)])  43.7 us
    pallas_call x3, Pallas kernels, schur_update(): pl.pallas_call(functools.partial(schur_update_kernel, count, len(bases),...  39.7 us
    ppermute x8, starting transfers between devices, hop(): lax.ppermute(value, 'tile', [(2 * a + c, 2 * b + c) for a, b in pairs for...  18.3 us
    ppermute x5, starting transfers between devices, handed(): return lax.ppermute(value, 'tm', [(t, t + 1) for t in range(count - 1)])  15.7 us
    dot_general x1, matrix products, nn(): lax.dot_general(left, right, (((1,), (0,)), ((), ())), precision=lax.Prec...  11.6 us
  transfers between devices with their start and end apart: 21, of which 8 were waited for; matrix products, arithmetic and copies ran while one was open for 15% of the time, Pallas kernels for 36%

profile of v2, /device:TPU:19, one launch (start us, length us, event | category | flops | bytes accessed | tf_op | source)
XLA Modules:
  0.0 352.1 jit_solution(16302522353105664170)
XLA Ops:
  0.6 3.2 slice.37.refs_0_.rest_0_
  9.0 3.2 maximum_maximum_fusion
  16.7 4.0 %fusion.10 = (f32[128,4096]{1,0:T(8,128)}, f32[128,4096]{1,0:T(8,128)S(1)}) fusion(f32[512,4096]{1,0:T(8,128)} %param.8), kind=kLoop, calls=%fused_computation.27 | loop fusion | bytes 8388608 | tf_op jit(solution)/shard_map/slice | solution.py:366
  20.7 30.7 %collective-permute-done.1.refs_2_.rest_2_ = f32[512,1024]{1,0:T(8,128)S(1)} collective-permute-done((f32[512,1024]{1,0:T(8,128)}, f32[512,1024]{1,0:T(8,128)S(1)}, u32[]{:S(2)}, u32[]{:S(2)}) %collective-permute-start.1) | collective-permute-done | bytes 2097184 | tf_op jit(solution)/shard_map/ppermute | solution.py:300
  54.7 7.3 %collective-permute-done.4.rest_2_.rest_1_ = f32[528,1024]{1,0:T(8,128)} collective-permute-done((f32[528,1024]{1,0:T(8,128)}, f32[528,1024]{1,0:T(8,128)}, u32[]{:S(2)}, u32[]{:S(2)}) %collective-permute-start.4) | collective-permute-done | bytes 2162720 | tf_op jit(solution)/shard_map/ppermute | solution.py:288
  62.0 4.0 %collective-permute-start.5 = (f32[128,4096]{1,0:T(8,128)S(1)}, f32[128,4096]{1,0:T(8,128)S(1)}, u32[]{:S(2)}, u32[]{:S(2)}) collective-permute-start(f32[128,4096]{1,0:T(8,128)S(1)} %get-tuple-element.35), channel_id=1, source_target_pairs={{0,8},{8,16},{16,24},{1,9},{9,17},{17,25},{2,10},{10,18},{18,26},{... | collective-permute-start | bytes 6291464 | tf_op jit(solution)/shard_map/ppermute | solution.py:288
  70.2 4.7 %slice.43 = f32[256,4096]{1,0:T(8,128)} slice(f32[512,4096]{1,0:T(8,128)} %param.8), slice={[128:384], [0:4096]} | slice | bytes 8388608 | tf_op jit(solution)/shard_map/slice | solution.py:335
  74.8 25.1 %collective-permute-done.3.refs_4_.rest_4_ = f32[512,1024]{1,0:T(8,128)} collective-permute-done((f32[512,1024]{1,0:T(8,128)S(1)}, f32[512,1024]{1,0:T(8,128)}, u32[]{:S(2)}, u32[]{:S(2)}) %collective-permute-start.3) | collective-permute-done | bytes 2097184 | tf_op jit(solution)/shard_map/ppermute | solution.py:300
  99.9 9.3 %collective-permute-done.5.rest_0_ = f32[128,4096]{1,0:T(8,128)S(1)} collective-permute-done((f32[128,4096]{1,0:T(8,128)S(1)}, f32[128,4096]{1,0:T(8,128)S(1)}, u32[]{:S(2)}, u32[]{:S(2)}) %collective-permute-start.5) | collective-permute-done | bytes 2097184 | tf_op jit(solution)/shard_map/ppermute | solution.py:288
  110.6 4.8 %collective-permute-start.10 = (f32[256,4096]{1,0:T(8,128)}, f32[256,4096]{1,0:T(8,128)}, u32[]{:S(2)}, u32[]{:S(2)}) collective-permute-start(f32[256,4096]{1,0:T(8,128)} %slice.43), channel_id=1, source_target_pairs={{0,8},{8,16},{16,24},{1,9},{9,17},{17,25},{2,10},{10,18},{18,26},{... | collective-permute-start | bytes 12582920 | tf_op jit(solution)/shard_map/ppermute | solution.py:288
  119.8 5.5 %collective-permute-start.9 = (f32[512,1024]{1,0:T(8,128)}, f32[512,1024]{1,0:T(8,128)}, u32[]{:S(2)}, u32[]{:S(2)}) collective-permute-start(f32[512,1024]{1,0:T(8,128)} %slice.37.refs_0_.rest_0_), channel_id=1, source_target_pairs={{2,6},{3,7},{4,0},{5,1},{10,14},{11,15},{12,8},{13,9},{18,22},{19,... | collective-permute-start | bytes 6291464 | tf_op jit(solution)/shard_map/ppermute | solution.py:300
  127.0 49.4 %shard_map.109 = f32[1024,1024]{1,0:T(8,128)} custom-call(s32[2]{0:T(128)S(1)} %pad_add_fusion.1.at_ref, f32[512,1024]{1,0:T(8,128)} %slice.37.refs_0_.rest_0_, f32[512,1024]{1,0:T(8,128)} %collective-permute-done.refs_1_.rest_1_, f32[512,1024]{1,0:T(8,128)S(1)} %collective-permute-done.1.refs_2_.rest_2_, f32[512,1024]{1,0:T(8,128)S(1)} %copy-done.5, ...), custom_call_target="tpu_custom_call" | custom-call | flops 1000000 | bytes 65536 | tf_op jit(solution)/shard_map/pallas_call | solution.py:130
  176.4 10.4 %fusion.1.solved_ref = f32[1056,1024]{1,0:T(8,128)S(1)} fusion(f32[1024,1024]{1,0:T(8,128)} %shard_map.109, f32[32,1024]{1,0:T(8,128)S(1)} %slice-done, f32[512,1024]{1,0:T(8,128)S(1)} %copy-done.8, f32[512,1024]{1,0:T(8,128)} %slice.37.refs_0_.rest_0_), kind=kOutput, calls=%fused_computation.3 | convolution fusion | flops 6645940224 | bytes 12845056 | tf_op jit(solution)/shard_map/dot_general | solution.py:279
  189.1 11.6 %fusion = (bf16[1056,1024]{1,0:T(8,128)(2,1)}, bf16[1056,1024]{1,0:T(8,128)(2,1)}, f32[1056,1024]{1,0:T(8,128)S(1)}) fusion(f32[1056,1024]{1,0:T(8,128)} %copy-done.7, f32[1024,1024]{1,0:T(8,128)} %shard_map.109), kind=kOutput, calls=%fused_computation.2 | convolution fusion | flops 6648102912 | bytes 17170432 | tf_op jit(solution)/shard_map/dot_general | solution.py:283
  204.5 7.3 %collective-permute-done.9 = f32[512,1024]{1,0:T(8,128)} collective-permute-done((f32[512,1024]{1,0:T(8,128)}, f32[512,1024]{1,0:T(8,128)}, u32[]{:S(2)}, u32[]{:S(2)}) %collective-permute-start.9) | collective-permute-done | bytes 2097184 | tf_op jit(solution)/shard_map/ppermute | solution.py:300
  211.8 3.6 %broadcast_select_fusion.1 = f32[528,1024]{1,0:T(8,128)} fusion(f32[528,1024]{1,0:T(8,128)} %collective-permute-done.4.rest_2_.rest_1_, f32[528,1024]{1,0:T(8,128)} %collective-permute-done.8.rest_4_.rest_3_, pred[]{:T(512)S(6)} %or.3), kind=kLoop, calls=%fused_computation.17 | loop fusion | flops 540672 | bytes 6488065 | tf_op jit(solution)/shard_map/jit(_where)/select_n | solution.py:347
  215.4 4.3 %collective-permute-start.13 = (f32[528,1024]{1,0:T(8,128)}, f32[528,1024]{1,0:T(8,128)}, u32[]{:S(2)}, u32[]{:S(2)}) collective-permute-start(f32[528,1024]{1,0:T(8,128)} %broadcast_select_fusion.1), channel_id=1, source_target_pairs={{0,2},{1,3},{4,6},{5,7},{6,4},{7,5},{2,0},{3,1},{8,10},{9,11},{12,... | collective-permute-start | bytes 6488072 | tf_op jit(solution)/shard_map/ppermute | solution.py:300
  224.7 32.2 %shard_map.110 = (f32[512,4096]{1,0:T(8,128)}, f32[512,4096]{1,0:T(8,128)}, f32[32,4096]{1,0:T(8,128)}) custom-call(s32[7]{0:T(128)S(1)} %stack.77.at_ref, bf16[1056,1024]{1,0:T(8,128)(2,1)} %get-tuple-element.67.high_ref, bf16[1056,1024]{1,0:T(8,128)(2,1)} %get-tuple-element.66.low_ref, f32[1056,1024]{1,0:T(8,128)} %copy-done.7, f32[512,4096]{1,0:T(8,128)} %a_ref.3, ...), custom_call_target="tpu_custom_call" | custom-call | flops 1000000 | bytes 65536 | tf_op jit(solution)/shard_map/pallas_call | solution.py:215
  256.9 14.4 %shard_map.111 = (f32[512,4096]{1,0:T(8,128)}, f32[512,4096]{1,0:T(8,128)}, f32[32,4096]{1,0:T(8,128)}) custom-call(s32[3]{0:T(128)S(1)} %pad_add_fusion.at_ref, bf16[1056,1024]{1,0:T(8,128)(2,1)} %get-tuple-element.67.high_ref, bf16[1056,1024]{1,0:T(8,128)(2,1)} %get-tuple-element.66.low_ref, ...), custom_call_target="tpu_custom_call", output_to_operand_aliasing={{0}: (9, {}), {1}: (10, {}), {2}: (11, {})} | custom-call | flops 1000000 | bytes 65536 | tf_op jit(solution)/shard_map/pallas_call | solution.py:215
  279.1 17.8 %shard_map.112 = (f32[512,4096]{1,0:T(8,128)}, f32[32,4096]{1,0:T(8,128)}) custom-call(s32[6]{0:T(128)S(1)} %stack.79.at_ref, bf16[544,1024]{1,0:T(8,128)(2,1)S(1)} %get-tuple-element.69.high_ref, bf16[544,1024]{1,0:T(8,128)(2,1)S(1)} %get-tuple-element.68.low_ref, f32[128,4096]{1,0:T(8,128)S(1)} %copy-done.2, f32[256,4096]{1,0:T(8,128)} %collective-permute-done.10.rest_1_, ...), custom_call_target="tpu_custom_call" | custom-call | flops 1000000 | bytes 65536 | tf_op jit(solution)/shard_map/pallas_call | solution.py:266
  297.0 27.1 %collective-permute-done.15.rest_0_.rest_2_ = f32[128,4096]{1,0:T(8,128)} collective-permute-done((f32[128,4096]{1,0:T(8,128)}, f32[128,4096]{1,0:T(8,128)}, u32[]{:S(2)}, u32[]{:S(2)}) %collective-permute-start.15) | collective-permute-done | bytes 2097184 | tf_op jit(solution)/shard_map/ppermute | solution.py:288
  324.1 3.6 %broadcast_select_fusion.rest_3_ = f32[528,1024]{1,0:T(8,128)} fusion(f32[528,1024]{1,0:T(8,128)} %collective-permute-done.16, f32[528,1024]{1,0:T(8,128)} %collective-permute-done.14, pred[]{:T(512)S(6)} %or.3), kind=kLoop, calls=%fused_computation.16 | loop fusion | flops 540672 | bytes 6488065 | tf_op jit(solution)/shard_map/jit(_where)/select_n | solution.py:374
  330.0 12.4 %shard_map.113.rest_5_ = f32[512,4096]{1,0:T(8,128)} custom-call(s32[6]{0:T(128)S(1)} %stack.79.at_ref, bf16[544,1024]{1,0:T(8,128)(2,1)S(1)} %get-tuple-element.69.high_ref, bf16[544,1024]{1,0:T(8,128)(2,1)S(1)} %get-tuple-element.68.low_ref, f32[128,4096]{1,0:T(8,128)} %collective-permute-done.15.rest_0_.rest_2_, ...), custom_call_target="tpu_custom_call", output_to_operand_aliasing={{}: (10, {})} | custom-call | flops 1000000 | bytes 65536 | tf_op jit(solution)/shard_map/pallas_call | solution.py:266
  342.5 9.4 %shard_map.114 = (f32[512,4096]{1,0:T(8,128)}, f32[32,4096]{1,0:T(8,128)}) custom-call(s32[2]{0:T(128)S(1)} %pad_add_fusion.2.at_ref, bf16[544,1024]{1,0:T(8,128)(2,1)S(1)} %get-tuple-element.69.high_ref, bf16[544,1024]{1,0:T(8,128)(2,1)S(1)} %get-tuple-element.68.low_ref, f32[128,4096]{1,0:T(8,128)S(1)} %copy-done.3, ...), custom_call_target="tpu_custom_call", output_to_operand_aliasing={{0}: (8, {}), {1}: (9, {})} | custom-call | flops 1000000 | bytes 65536 | tf_op jit(solution)/shard_map/pallas_call | solution.py:266
  (70 shorter events, 45.6 us)
Async XLA Ops:
  3.8 47.6 %collective-permute-start.1 = (f32[512,1024]{1,0:T(8,128)}, f32[512,1024]{1,0:T(8,128)S(1)}, u32[]{:S(2)}, u32[]{:S(2)}) collective-permute-start(f32[512,1024]{1,0:T(8,128)} %slice.37.refs_0_.rest_0_), channel_id=1, source_target_pairs={{0,4},{1,5},{6,2},{7,3},{4,6},{5,7},{2,0},{3,1},{8,12},{9,13},{14,... | collective-permute-start | bytes 6291464 | tf_op jit(solution)/shard_map/ppermute | solution.py:300
  12.2 49.8 %collective-permute-start.4 = (f32[528,1024]{1,0:T(8,128)}, f32[528,1024]{1,0:T(8,128)}, u32[]{:S(2)}, u32[]{:S(2)}) collective-permute-start(f32[528,1024]{1,0:T(8,128)} %maximum_maximum_fusion), channel_id=1, source_target_pairs={{0,8},{8,16},{16,24},{1,9},{9,17},{17,25},{2,10},{10,18},{18,26},{... | collective-permute-start | bytes 6488072 | tf_op jit(solution)/shard_map/ppermute | solution.py:288
  15.4 52.9 %collective-permute-start = (f32[512,1024]{1,0:T(8,128)}, f32[512,1024]{1,0:T(8,128)}, u32[]{:S(2)}, u32[]{:S(2)}) collective-permute-start(f32[512,1024]{1,0:T(8,128)} %slice.37.refs_0_.rest_0_), channel_id=1, source_target_pairs={{0,1},{1,0},{2,3},{3,2},{4,5},{5,4},{6,7},{7,6},{8,9},{9,8},{10,11... | collective-permute-start | bytes 6291464 | tf_op jit(solution)/shard_map/ppermute | solution.py:304
  51.4 74.0 %copy-start = (f32[512,1024]{1,0:T(8,128)}, f32[512,1024]{1,0:T(8,128)S(1)}, u32[]{:S(2)}) copy-start(f32[512,1024]{1,0:T(8,128)S(1)} %collective-permute-done.1.refs_2_.rest_2_) | copy-start | bytes 6291460
  54.2 45.7 %collective-permute-start.3 = (f32[512,1024]{1,0:T(8,128)S(1)}, f32[512,1024]{1,0:T(8,128)}, u32[]{:S(2)}, u32[]{:S(2)}) collective-permute-start(f32[512,1024]{1,0:T(8,128)S(1)} %broadcast_select_fusion.3), channel_id=1, source_target_pairs={{0,2},{1,3},{4,6},{5,7},{6,4},{7,5},{2,0},{3,1},{8,10},{9,11},{12,... | collective-permute-start | bytes 6291464 | tf_op jit(solution)/shard_map/ppermute | solution.py:300
  62.0 47.2 %collective-permute-start.5 = (f32[128,4096]{1,0:T(8,128)S(1)}, f32[128,4096]{1,0:T(8,128)S(1)}, u32[]{:S(2)}, u32[]{:S(2)}) collective-permute-start(f32[128,4096]{1,0:T(8,128)S(1)} %get-tuple-element.35), channel_id=1, source_target_pairs={{0,8},{8,16},{16,24},{1,9},{9,17},{17,25},{2,10},{10,18},{18,26},{... | collective-permute-start | bytes 6291464 | tf_op jit(solution)/shard_map/ppermute | solution.py:288
  66.0 49.4 %collective-permute-start.2 = (f32[512,1024]{1,0:T(8,128)S(1)}, f32[512,1024]{1,0:T(8,128)S(1)}, u32[]{:S(2)}, u32[]{:S(2)}) collective-permute-start(f32[512,1024]{1,0:T(8,128)S(1)} %collective-permute-done.1.refs_2_.rest_2_), channel_id=1, source_target_pairs={{0,1},{1,0},{2,3},{3,2},{4,5},{5,4},{6,7},{7,6},{8,9},{9,8},{10,11... | collective-permute-start | bytes 6291464 | tf_op jit(solution)/shard_map/ppermute | solution.py:304
  68.2 49.4 %collective-permute-start.6 = (f32[512,1024]{1,0:T(8,128)}, f32[512,1024]{1,0:T(8,128)}, u32[]{:S(2)}, u32[]{:S(2)}) collective-permute-start(f32[512,1024]{1,0:T(8,128)} %slice.37.refs_0_.rest_0_), channel_id=1, source_target_pairs={{2,4},{3,5},{4,2},{5,3},{10,12},{11,13},{12,10},{13,11},{18,20},{1... | collective-permute-start | bytes 6291464 | tf_op jit(solution)/shard_map/ppermute | solution.py:300
  110.6 101.2 %collective-permute-start.10 = (f32[256,4096]{1,0:T(8,128)}, f32[256,4096]{1,0:T(8,128)}, u32[]{:S(2)}, u32[]{:S(2)}) collective-permute-start(f32[256,4096]{1,0:T(8,128)} %slice.43), channel_id=1, source_target_pairs={{0,8},{8,16},{16,24},{1,9},{9,17},{17,25},{2,10},{10,18},{18,26},{... | collective-permute-start | bytes 12582920 | tf_op jit(solution)/shard_map/ppermute | solution.py:288
  117.7 7.7 %collective-permute-start.7 = (f32[512,1024]{1,0:T(8,128)}, f32[512,1024]{1,0:T(8,128)}, u32[]{:S(2)}, u32[]{:S(2)}) collective-permute-start(f32[512,1024]{1,0:T(8,128)} %collective-permute-done.3.refs_4_.rest_4_), channel_id=1, source_target_pairs={{0,1},{1,0},{2,3},{3,2},{4,5},{5,4},{6,7},{7,6},{8,9},{9,8},{10,11... | collective-permute-start | bytes 6291464 | tf_op jit(solution)/shard_map/ppermute | solution.py:304
  119.8 92.0 %collective-permute-start.8 = (f32[528,1024]{1,0:T(8,128)}, f32[528,1024]{1,0:T(8,128)}, u32[]{:S(2)}, u32[]{:S(2)}) collective-permute-start(f32[528,1024]{1,0:T(8,128)} %collective-permute-done.4.rest_2_.rest_1_), channel_id=1, source_target_pairs={{0,4},{1,5},{6,2},{7,3},{4,6},{5,7},{2,0},{3,1},{8,12},{9,13},{14,... | collective-permute-start | bytes 6488072 | tf_op jit(solution)/shard_map/ppermute | solution.py:300
  119.8 92.0 %collective-permute-start.9 = (f32[512,1024]{1,0:T(8,128)}, f32[512,1024]{1,0:T(8,128)}, u32[]{:S(2)}, u32[]{:S(2)}) collective-permute-start(f32[512,1024]{1,0:T(8,128)} %slice.37.refs_0_.rest_0_), channel_id=1, source_target_pairs={{2,6},{3,7},{4,0},{5,1},{10,14},{11,15},{12,8},{13,9},{18,22},{19,... | collective-permute-start | bytes 6291464 | tf_op jit(solution)/shard_map/ppermute | solution.py:300
  127.0 49.4 %slice-start = ((f32[32,4096]{1,0:T(8,128)}), f32[32,1024]{1,0:T(8,128)S(1)}, s32[]{:S(2)}) async-start(f32[32,4096]{1,0:T(8,128)} %r_ref.3), calls=%async_computation | async-start | bytes 262144 | tf_op jit(solution)/shard_map/slice | solution.py:319
  127.0 49.4 %copy-start.8 = (f32[512,1024]{1,0:T(8,128)S(1)}, f32[512,1024]{1,0:T(8,128)}, u32[]{:S(2)}) copy-start(f32[512,1024]{1,0:T(8,128)} %slice.38) | copy-start | bytes 6291460
  202.6 68.7 %collective-permute-start.12 = (f32[552,1024]{1,0:T(8,128)}, f32[552,1024]{1,0:T(8,128)}, u32[]{:S(2)}, u32[]{:S(2)}) collective-permute-start(f32[552,1024]{1,0:T(8,128)} %select_maximum_fusion), channel_id=1, source_target_pairs={{0,8},{8,16},{16,24},{1,9},{9,17},{17,25},{2,10},{10,18},{18,26},{... | collective-permute-start | bytes 6782984 | tf_op jit(solution)/shard_map/ppermute | solution.py:288
  215.4 55.9 %collective-permute-start.13 = (f32[528,1024]{1,0:T(8,128)}, f32[528,1024]{1,0:T(8,128)}, u32[]{:S(2)}, u32[]{:S(2)}) collective-permute-start(f32[528,1024]{1,0:T(8,128)} %broadcast_select_fusion.1), channel_id=1, source_target_pairs={{0,2},{1,3},{4,6},{5,7},{6,4},{7,5},{2,0},{3,1},{8,10},{9,11},{12,... | collective-permute-start | bytes 6488072 | tf_op jit(solution)/shard_map/ppermute | solution.py:300
  219.7 51.6 %collective-permute-start.14 = (f32[528,1024]{1,0:T(8,128)}, f32[528,1024]{1,0:T(8,128)}, u32[]{:S(2)}, u32[]{:S(2)}) collective-permute-start(f32[528,1024]{1,0:T(8,128)} %collective-permute-done.4.rest_2_.rest_1_), channel_id=1, source_target_pairs={{2,4},{3,5},{4,2},{5,3},{10,12},{11,13},{12,10},{13,11},{18,20},{1... | collective-permute-start | bytes 6488072 | tf_op jit(solution)/shard_map/ppermute | solution.py:300
  223.7 33.3 %collective-permute-start.11 = (f32[512,1024]{1,0:T(8,128)S(1)}, f32[512,1024]{1,0:T(8,128)}, u32[]{:S(2)}, u32[]{:S(2)}) collective-permute-start(f32[512,1024]{1,0:T(8,128)S(1)} %broadcast_select_fusion.2.rest_0_), channel_id=1, source_target_pairs={{0,1},{1,0},{2,3},{3,2},{4,5},{5,4},{6,7},{7,6},{8,9},{9,8},{10,11... | collective-permute-start | bytes 6291464 | tf_op jit(solution)/shard_map/ppermute | solution.py:304
  224.6 54.3 %collective-permute-start.18 = (f32[528,1024]{1,0:T(8,128)}, f32[528,1024]{1,0:T(8,128)}, u32[]{:S(2)}, u32[]{:S(2)}) collective-permute-start(f32[528,1024]{1,0:T(8,128)} %collective-permute-done.8.rest_4_.rest_3_), channel_id=1, source_target_pairs={{0,1},{1,0},{2,3},{3,2},{4,5},{5,4},{6,7},{7,6},{8,9},{9,8},{10,11... | collective-permute-start | bytes 6488072 | tf_op jit(solution)/shard_map/ppermute | solution.py:304
  271.4 7.6 %collective-permute-start.17 = (f32[528,1024]{1,0:T(8,128)}, f32[528,1024]{1,0:T(8,128)}, u32[]{:S(2)}, u32[]{:S(2)}) collective-permute-start(f32[528,1024]{1,0:T(8,128)} %collective-permute-done.4.rest_2_.rest_1_), channel_id=1, source_target_pairs={{0,1},{1,0},{2,3},{3,2},{4,5},{5,4},{6,7},{7,6},{8,9},{9,8},{10,11... | collective-permute-start | bytes 6488072 | tf_op jit(solution)/shard_map/ppermute | solution.py:304
  271.5 7.7 %collective-permute-start.19 = (f32[528,1024]{1,0:T(8,128)}, f32[528,1024]{1,0:T(8,128)}, u32[]{:S(2)}, u32[]{:S(2)}) collective-permute-start(f32[528,1024]{1,0:T(8,128)} %collective-permute-done.13.rest_6_.rest_5_), channel_id=1, source_target_pairs={{0,1},{1,0},{2,3},{3,2},{4,5},{5,4},{6,7},{7,6},{8,9},{9,8},{10,11... | collective-permute-start | bytes 6488072 | tf_op jit(solution)/shard_map/ppermute | solution.py:304
  271.9 52.1 %collective-permute-start.16 = (f32[528,1024]{1,0:T(8,128)}, f32[528,1024]{1,0:T(8,128)}, u32[]{:S(2)}, u32[]{:S(2)}) collective-permute-start(f32[528,1024]{1,0:T(8,128)} %collective-permute-done.4.rest_2_.rest_1_), channel_id=1, source_target_pairs={{2,6},{3,7},{4,0},{5,1},{10,14},{11,15},{12,8},{13,9},{18,22},{19,... | collective-permute-start | bytes 6488072 | tf_op jit(solution)/shard_map/ppermute | solution.py:300
  274.7 49.4 %collective-permute-start.15 = (f32[128,4096]{1,0:T(8,128)}, f32[128,4096]{1,0:T(8,128)}, u32[]{:S(2)}, u32[]{:S(2)}) collective-permute-start(f32[128,4096]{1,0:T(8,128)} %get-tuple-element.53), channel_id=1, source_target_pairs={{0,8},{8,16},{16,24},{1,9},{9,17},{17,25},{2,10},{10,18},{18,26},{... | collective-permute-start | bytes 6291464 | tf_op jit(solution)/shard_map/ppermute | solution.py:288
  327.7 14.8 %collective-permute-start.20 = (f32[528,1024]{1,0:T(8,128)}, f32[528,1024]{1,0:T(8,128)}, u32[]{:S(2)}, u32[]{:S(2)}) collective-permute-start(f32[528,1024]{1,0:T(8,128)} %broadcast_select_fusion.rest_3_), channel_id=1, source_target_pairs={{0,1},{1,0},{2,3},{3,2},{4,5},{5,4},{6,7},{7,6},{8,9},{9,8},{10,11... | collective-permute-start | bytes 6488072 | tf_op jit(solution)/shard_map/ppermute | solution.py:304
  (8 other events, 42.9 us)

commit v3 on v2

--- a/solution.py
+++ b/solution.py
@@ -160,17 +160,26 @@
 LIGHT = pl.CostEstimate(flops=1_000_000, bytes_accessed=1 << 16, transcendentals=0)
 
 
-def fetch(step, sources, buffer_ref, sems):
-    for i in range(len(sources)):
-        @pl.when(step == i)
-        def _(i=i):
-            copies = [pltpu.make_async_copy(sources[j], buffer_ref.at[j % 2], sems.at[j % 2])
-                      for j in (i, i + 1) if j < len(sources)]
-            if i == 0:
-                copies[0].start()
-            if len(copies) > 1:
-                copies[1].start()
-            copies[0].wait()
+def fetch(step, sources, buffer_ref, sems, flag=None):
+    count = len(sources) if flag is None else len(sources) // 2
+
+    def run(chosen):
+        for i in range(count):
+            @pl.when(step == i)
+            def _(i=i):
+                copies = [pltpu.make_async_copy(chosen[j], buffer_ref.at[j % 2], sems.at[j % 2])
+                          for j in (i, i + 1) if j < count]
+                if i == 0:
+                    copies[0].start()
+                if len(copies) > 1:
+                    copies[1].start()
+                copies[0].wait()
+
+    if flag is None:
+        run(sources)
+    else:
+        pl.when(flag != 0)(lambda: run(sources[:count]))
+        pl.when(flag == 0)(lambda: run(sources[count:]))
 
 
 def panel_update_kernel(count, at_ref, high_ref, low_ref, solved_ref, a_ref, c_ref, r_ref, *rest):
@@ -225,54 +234,69 @@
     )(*args)
 
 
-def schur_update_kernel(count, parts, arrow, at_ref, high_ref, low_ref, *rest):
-    bases, sources, (*outs, buffer_ref, sems) = rest[:parts], rest[parts:parts + count], rest[-2 - (2 if arrow else 1):]
+def schur_update_kernel(count, parts, flagged, at_ref, high_ref, low_ref, *rest):
+    bases, sources, (d_out, b_out, buffer_ref, sems) = rest[:parts], rest[parts:parts + count], rest[-4:]
     step = pl.program_id(0)
-    height, rows = outs[0].shape
-    fetch(step, sources, buffer_ref, sems)
+    height, rows = d_out.shape
+    fetch(step, sources, buffer_ref, sems, at_ref[count // 2] if flagged else None)
     x_ref = buffer_ref.at[step % 2]
     x = halves(x_ref[:rows])
     total = product((high_ref[:height], low_ref[:height]), x)
     start = 0
     for base in bases:
         end = start + base.shape[0]
-        outs[0][start:end] = base[...] - total[start:end]
+        d_out[start:end] = base[...] - total[start:end]
         start = end
-    if arrow:
-        base = jnp.concatenate([x_ref[rows:, :rows], x_ref[rows:, rows:2 * rows]], axis=0)
-        outs[1][...] = base - product((high_ref[rows:], low_ref[rows:]), x)
-
-
-def schur_update(at, weights, bases, blocks, before, row_at=0, arrow=True):
+    if start < height:
+        d_out[start:] = -total[start:]
+    base = jnp.concatenate([x_ref[rows:, :rows], x_ref[rows:, rows:2 * rows]], axis=0)
+    b_out[...] = base - product((high_ref[rows:], low_ref[rows:]), x)
+
+
+def schur_update(at, weights, bases, blocks, before, flagged=False):
     rows, pivots = blocks[0].shape[0] - 16, blocks[0].shape[1]
     arrows, cols = weights[0].shape[0] - rows, bases[0].shape[1]
-    height = sum(base.shape[0] for base in bases)
     count = len(blocks)
+    steps = count // 2 if flagged else count
     whole = pl.BlockSpec(memory_space=pl.ANY)
-    fixed = pl.BlockSpec((rows + arrows if arrow else height, pivots), lambda i, at: (row_at, 0))
-    in_specs = [fixed] * 2 + [pl.BlockSpec((base.shape[0], rows), lambda i, at: (0, at[i])) for base in bases]
-    in_specs += [whole] * count
+    moving = lambda tall: pl.BlockSpec((tall, rows), lambda i, at: (0, at[i]))
+    in_specs = [pl.BlockSpec((rows + arrows, pivots), lambda i, at: (0, 0))] * 2
+    in_specs += [moving(base.shape[0]) for base in bases] + [whole] * count
     args = [at, *weights, *bases, *blocks]
-    out_shape = [jax.ShapeDtypeStruct((rows, cols), jnp.float32)]
-    out_specs = [pl.BlockSpec((height, rows), lambda i, at: (row_at, at[i]))]
-    if arrow:
-        out_shape.append(jax.ShapeDtypeStruct((arrows, cols), jnp.float32))
-        out_specs.append(pl.BlockSpec((arrows, rows), lambda i, at: (0, at[i])))
     aliases = {}
     if before is not None:
-        aliases = {len(args) + i: i for i in range(len(before))}
-        in_specs += [whole] * len(before)
+        aliases = {len(args) + i: i for i in range(2)}
+        in_specs += [whole] * 2
         args += list(before)
     return pl.pallas_call(
-        functools.partial(schur_update_kernel, count, len(bases), arrow),
-        out_shape=out_shape,
+        functools.partial(schur_update_kernel, count, len(bases), flagged),
+        out_shape=[jax.ShapeDtypeStruct((rows, cols), jnp.float32), jax.ShapeDtypeStruct((arrows, cols), jnp.float32)],
         grid_spec=pltpu.PrefetchScalarGridSpec(
-            num_scalar_prefetch=1, grid=(count,), in_specs=in_specs, out_specs=out_specs,
+            num_scalar_prefetch=1, grid=(steps,), in_specs=in_specs, out_specs=[moving(rows), moving(arrows)],
             scratch_shapes=[pltpu.VMEM((2, rows + 16, pivots), jnp.float32), pltpu.SemaphoreType.DMA((2,))]),
         input_output_aliases=aliases,
         compiler_params=pltpu.CompilerParams(vmem_limit_bytes=48 << 20),
         cost_estimate=LIGHT,
     )(*args)
+
+
+def add_rows_kernel(at_ref, base_ref, before_ref, out_ref):
+    out_ref[...] = base_ref[...] + before_ref[...]
+
+
+def add_rows(at, base, before, width):
+    tall = base.shape[0]
+    row_at = before.shape[0] // tall - 1
+    bottom = pl.BlockSpec((tall, width), lambda i, at: (row_at, at[i]))
+    return pl.pallas_call(
+        add_rows_kernel,
+        out_shape=jax.ShapeDtypeStruct(before.shape, before.dtype),
+        grid_spec=pltpu.PrefetchScalarGridSpec(
+            num_scalar_prefetch=1, grid=(at.shape[0],),
+            in_specs=[pl.BlockSpec((tall, width), lambda i, at: (0, at[i])), bottom], out_specs=bottom),
+        input_output_aliases={2: 0},
+        cost_estimate=LIGHT,
+    )(at, base, before)
 
 
 def nt(left, right):
@@ -327,22 +351,22 @@
     past_c = handed(sent_c)
     o_own = sibling(panel_a)
     e2 = hop(jnp.where(edge, panel_a, e1), second)
-    e4 = hop(after(panel_a, e1, past_c, o_own), fourth)
+    e4 = hop(after(panel_a, e1, o_own), fourth)
     d1 = handed(after(next_diag[:near], past_c))
     o_e1 = sibling(e1)
     e3 = hop(after(panel_a, e2, e4), third)
     f1 = hop(after(past_c, e2, e4), first)
     d2 = handed(after(next_diag[near:end], e2, d1))
-    o_e2 = sibling(after(e2, d1, e4, o_own, o_e1))
+    o_e2 = sibling(after(e2, o_own, o_e1))
     pick = jnp.stack([jnp.where(chip == 0, 0, jnp.where(chip == 2, 1, 2)), core])
-    inverse = chain_picked(pick, [panel_a, o_own, e1, o_e1, e2, o_e2])
+    inverse = chain_picked(after(pick, d1), [panel_a, o_own, e1, o_e1, e2, o_e2])
     solved = nt(jnp.concatenate([panel_a, panel_c, panel_r]), inverse)
     weight = nn(solved, inverse)
 
     tip = arrow_tip - nt(solved[2 * rows:], solved[2 * rows:])
     tip = jnp.pad(tip.reshape(1, -1), ((0, 7), (0, pivots - arrows * arrows)))
     past_w = handed(jnp.concatenate([weight[rows:], tip]))
-    f1, e3, d2 = stage((f1, e3, d2), weight)
+    f1, e3 = stage((f1, e3), weight)
     r3 = jnp.where(edge, e3, e4)
     f2 = hop(jnp.where(edge, past_c, f1), second)
     f4 = hop(after(past_c, f1), fourth)
@@ -365,15 +389,15 @@
     f3 = hop(after(past_c, f4, f2), third)
     d3 = handed(after(next_diag[end:], past_w))
     past_tip = past_w[rows + arrows, :arrows * arrows].reshape(arrows, arrows)
-    o_f2, o_c = sibling(f2), sibling(after(past_c, f2))
+    o_f2, o_f4, o_c = sibling(f2), sibling(f4), sibling(after(past_c, f2))
     split = bf16_halves(past_w[:rows + arrows])
     blocks = [past_c, o_c, f1, o_f1, f2, o_f2]
     past_d, past_b = schur_update(table(early), split, [d1, d2], blocks, None)
     d3, f3 = stage((d3, f3), past_b)
-    past_d, = schur_update(table(early), split, [d3], blocks, [past_d], rows // near - 1, False)
-    s3 = jnp.where(edge, f3, f4)
-    gone = schur_update(table(late), split, [d1, d2, d3], [s3, sibling(s3)], [past_d, past_b])
-    return (*out, *gone, past_tip)
+    past_d = add_rows(table(early), d3, past_d, rows)
+    blocks = [f3, sibling(f3), f4, o_f4]
+    past_d, past_b = schur_update(table(late + [edge]), split, [d1, d2, d3], blocks, [past_d, past_b], True)
+    return (*out, past_d, past_b, past_tip)
 
 
 def local(diag_blocks, coupling, next_diag, arrow_now, arrow_next, arrow_tip):

time: 356 us -> 336 us (0.944)
  waiting for transfers between devices: 108 us -> 95.6 us
  Pallas kernels: 136 us -> 131 us
  other arithmetic: 19.2 us -> 15.5 us
    ppermute x5, waiting for transfers between devices: 43.7 us -> 23.2 us  [handed(): return lax.ppermute(value, 'tm', [(t, t + 1) for t in range(count - 1)])]
    pallas_call x3 -> x2, Pallas kernels: 39.7 us -> 29.7 us  [schur_update(): pl.pallas_call(functools.partial(schur_update_kernel, count, len(bases),...]
    ppermute x8, waiting for transfers between devices: 64.1 us -> 72.4 us  [hop(): lax.ppermute(value, 'tile', [(2 * a + c, 2 * b + c) for a, b in pairs for...]
    pallas_call x0 -> x1, Pallas kernels: none -> 5.53 us  [add_rows(): pl.pallas_call(add_rows_kernel, out_shape=jax.ShapeDtypeStruct(before.sha...]
    select_n x1 -> x0, other arithmetic: 3.58 us -> none  [local_line(): s3 = jnp.where(edge, f3, f4)]
    ppermute x8 -> x9, starting transfers between devices: 7.92 us -> 10.1 us  [sibling(): return lax.ppermute(value, 'tile', [(i, i ^ 1) for i in range(8)])]
  transfers between devices with their start and end apart: 21 -> 22, of which waited for: 8 -> 6; matrix products, arithmetic and copies ran while one was open for 15% -> 15% of each run, Pallas kernels for 36% -> 37%
where the time goes in v3:
time: 336 us; the launch traced here: 330 us
  Pallas kernels  131 us (39%)
  waiting for transfers between devices  95.6 us (28%)
  starting transfers between devices  44.8 us (13%)
  local copies, waits for them, and re-layouts  22.1 us (7%)
  matrix products  20 us (6%)
  other arithmetic  15.5 us (5%)
    ppermute x8, waiting for transfers between devices, hop(): lax.ppermute(value, 'tile', [(2 * a + c, 2 * b + c) for a, b in pairs for...  72.4 us
    pallas_call x1, Pallas kernels, chain_picked(): pl.pallas_call(chain_picked_kernel, out_shape=jax.ShapeDtypeStruct((n, n)...  49.3 us
    pallas_call x2, Pallas kernels, panel_update(): pl.pallas_call(functools.partial(panel_update_kernel, count), out_shape=[...  46.6 us
    pallas_call x2, Pallas kernels, schur_update(): pl.pallas_call(functools.partial(schur_update_kernel, count, len(bases),...  29.7 us
    ppermute x5, waiting for transfers between devices, handed(): return lax.ppermute(value, 'tm', [(t, t + 1) for t in range(count - 1)])  23.2 us
    ppermute x5, starting transfers between devices, handed(): return lax.ppermute(value, 'tm', [(t, t + 1) for t in range(count - 1)])  17.4 us
    ppermute x8, starting transfers between devices, hop(): lax.ppermute(value, 'tile', [(2 * a + c, 2 * b + c) for a, b in pairs for...  17.3 us
    dot_general x2, matrix products, nt(): lax.dot_general(left, right, (((1,), (1,)), ((), ())), precision=lax.Prec...  10.7 us
  transfers between devices with their start and end apart: 22, of which 6 were waited for; matrix products, arithmetic and copies ran while one was open for 15% of the time, Pallas kernels for 37%

profile of v3, /device:TPU:19, one launch (start us, length us, event | category | flops | bytes accessed | tf_op | source)
XLA Modules:
  0.0 330.2 jit_solution(5975019655089948118)
XLA Ops:
  0.6 3.2 slice.37.refs_0_.rest_0_
  6.1 3.2 slice.38
  10.0 3.2 maximum_maximum_fusion
  16.3 35.1 %collective-permute-done.3.refs_2_.rest_2_ = f32[512,1024]{1,0:T(8,128)S(1)} collective-permute-done((f32[512,1024]{1,0:T(8,128)}, f32[512,1024]{1,0:T(8,128)S(1)}, u32[]{:S(2)}, u32[]{:S(2)}) %collective-permute-start.3) | collective-permute-done | bytes 2097184 | tf_op jit(solution)/shard_map/ppermute | solution.py:324
  58.4 5.0 %fusion.10 = (f32[128,4096]{1,0:T(8,128)}, f32[128,4096]{1,0:T(8,128)}) fusion(f32[512,4096]{1,0:T(8,128)} %param.8), kind=kLoop, calls=%fused_computation.27 | loop fusion | bytes 8388608 | tf_op jit(solution)/shard_map/slice | solution.py:390
  64.1 4.0 %collective-permute-start.1 = (f32[128,4096]{1,0:T(8,128)}, f32[128,4096]{1,0:T(8,128)}, u32[]{:S(2)}, u32[]{:S(2)}) collective-permute-start(f32[128,4096]{1,0:T(8,128)} %get-tuple-element.35), channel_id=1, source_target_pairs={{0,8},{8,16},{16,24},{1,9},{9,17},{17,25},{2,10},{10,18},{18,26},{... | collective-permute-start | bytes 6291464 | tf_op jit(solution)/shard_map/ppermute | solution.py:312
  68.1 31.8 %collective-permute-done.5.refs_4_.rest_4_ = f32[512,1024]{1,0:T(8,128)} collective-permute-done((f32[512,1024]{1,0:T(8,128)S(1)}, f32[512,1024]{1,0:T(8,128)}, u32[]{:S(2)}, u32[]{:S(2)}) %collective-permute-start.5) | collective-permute-done | bytes 2097184 | tf_op jit(solution)/shard_map/ppermute | solution.py:324
  105.9 5.6 %collective-permute-start.9 = (f32[512,1024]{1,0:T(8,128)}, f32[512,1024]{1,0:T(8,128)}, u32[]{:S(2)}, u32[]{:S(2)}) collective-permute-start(f32[512,1024]{1,0:T(8,128)} %slice.37.refs_0_.rest_0_), channel_id=1, source_target_pairs={{2,6},{3,7},{4,0},{5,1},{10,14},{11,15},{12,8},{13,9},{18,22},{19,... | collective-permute-start | bytes 6291464 | tf_op jit(solution)/shard_map/ppermute | solution.py:324
  111.5 4.7 %slice.43 = f32[256,4096]{1,0:T(8,128)} slice(f32[512,4096]{1,0:T(8,128)} %param.8), slice={[128:384], [0:4096]} | slice | bytes 8388608 | tf_op jit(solution)/shard_map/slice | solution.py:359
  116.2 3.1 collective-permute-start.11
  121.0 49.3 %shard_map.109 = f32[1024,1024]{1,0:T(8,128)} custom-call(s32[2]{0:T(128)S(1)} %pad_add_fusion.2.at_ref, f32[512,1024]{1,0:T(8,128)} %slice.37.refs_0_.rest_0_, f32[512,1024]{1,0:T(8,128)} %collective-permute-done.2.refs_1_.rest_1_, f32[512,1024]{1,0:T(8,128)S(1)} %collective-permute-done.3.refs_2_.rest_2_, f32[512,1024]{1,0:T(8,128)S(1)} %copy-done.2, ...), custom_call_target="tpu_custom_call" | custom-call | flops 1000000 | bytes 65536 | tf_op jit(solution)/shard_map/pallas_call | solution.py:130
  170.3 10.5 %fusion.1.solved_ref = f32[1056,1024]{1,0:T(8,128)S(1)} fusion(f32[1024,1024]{1,0:T(8,128)} %shard_map.109, f32[32,1024]{1,0:T(8,128)S(1)} %slice-done, f32[512,1024]{1,0:T(8,128)S(1)} %copy-done.6, f32[512,1024]{1,0:T(8,128)} %slice.37.refs_0_.rest_0_), kind=kOutput, calls=%fused_computation.3 | convolution fusion | flops 6645940224 | bytes 12845056 | tf_op jit(solution)/shard_map/dot_general | solution.py:303
  180.9 9.3 %fusion = (bf16[1056,1024]{1,0:T(8,128)(2,1)}, bf16[1056,1024]{1,0:T(8,128)(2,1)}, f32[1056,1024]{1,0:T(8,128)S(1)}) fusion(f32[1056,1024]{1,0:T(8,128)S(1)} %fusion.1.solved_ref, f32[1024,1024]{1,0:T(8,128)S(1)} %copy-done.7), kind=kOutput, calls=%fused_computation.2 | convolution fusion | flops 6648102912 | bytes 17170432 | tf_op jit(solution)/shard_map/dot_general | solution.py:307
  192.7 3.1 collective-permute-start.12
  195.8 3.2 collective-permute-done.9
  199.1 3.6 %broadcast_select_fusion = f32[528,1024]{1,0:T(8,128)} fusion(f32[528,1024]{1,0:T(8,128)} %collective-permute-done.rest_2_, f32[528,1024]{1,0:T(8,128)} %collective-permute-done.8.rest_4_, pred[]{:T(512)S(6)} %or.3), kind=kLoop, calls=%fused_computation.16 | loop fusion | flops 540672 | bytes 6488065 | tf_op jit(solution)/shard_map/jit(_where)/select_n | solution.py:371
  202.7 3.2 collective-permute-start.13
  213.3 32.2 %shard_map.110 = (f32[512,4096]{1,0:T(8,128)}, f32[512,4096]{1,0:T(8,128)}, f32[32,4096]{1,0:T(8,128)}) custom-call(s32[7]{0:T(128)S(1)} %stack.83.at_ref, bf16[1056,1024]{1,0:T(8,128)(2,1)} %get-tuple-element.67.high_ref, bf16[1056,1024]{1,0:T(8,128)(2,1)} %get-tuple-element.66.low_ref, f32[1056,1024]{1,0:T(8,128)} %copy-done.5, f32[512,4096]{1,0:T(8,128)} %a_ref.3, ...), custom_call_target="tpu_custom_call" | custom-call | flops 1000000 | bytes 65536 | tf_op jit(solution)/shard_map/pallas_call | solution.py:224
  245.5 14.4 %shard_map.111 = (f32[512,4096]{1,0:T(8,128)}, f32[512,4096]{1,0:T(8,128)}, f32[32,4096]{1,0:T(8,128)}) custom-call(s32[3]{0:T(128)S(1)} %pad_add_fusion.at_ref, bf16[1056,1024]{1,0:T(8,128)(2,1)} %get-tuple-element.67.high_ref, bf16[1056,1024]{1,0:T(8,128)(2,1)} %get-tuple-element.66.low_ref, ...), custom_call_target="tpu_custom_call", output_to_operand_aliasing={{0}: (9, {}), {1}: (10, {}), {2}: (11, {})} | custom-call | flops 1000000 | bytes 65536 | tf_op jit(solution)/shard_map/pallas_call | solution.py:224
  263.2 4.0 %collective-permute-start.15 = (f32[128,4096]{1,0:T(8,128)}, f32[128,4096]{1,0:T(8,128)}, u32[]{:S(2)}, u32[]{:S(2)}) collective-permute-start(f32[128,4096]{1,0:T(8,128)} %get-tuple-element.53), channel_id=1, source_target_pairs={{0,8},{8,16},{16,24},{1,9},{9,17},{17,25},{2,10},{10,18},{18,26},{... | collective-permute-start | bytes 6291464 | tf_op jit(solution)/shard_map/ppermute | solution.py:312
  269.9 20.3 %shard_map.112 = (f32[512,4096]{1,0:T(8,128)}, f32[32,4096]{1,0:T(8,128)}) custom-call(s32[6]{0:T(128)S(1)} %stack.87.at_ref, bf16[544,1024]{1,0:T(8,128)(2,1)S(1)} %get-tuple-element.69.high_ref, bf16[544,1024]{1,0:T(8,128)(2,1)S(1)} %get-tuple-element.68.low_ref, f32[128,4096]{1,0:T(8,128)} %collective-permute-done.1.rest_0_, ...), custom_call_target="tpu_custom_call" | custom-call | flops 1000000 | bytes 65536 | tf_op jit(solution)/shard_map/pallas_call | solution.py:271
  290.1 22.5 %collective-permute-done.15.base_ref.rest_2_ = f32[128,4096]{1,0:T(8,128)} collective-permute-done((f32[128,4096]{1,0:T(8,128)}, f32[128,4096]{1,0:T(8,128)}, u32[]{:S(2)}, u32[]{:S(2)}) %collective-permute-start.15) | collective-permute-done | bytes 2097184 | tf_op jit(solution)/shard_map/ppermute | solution.py:312
  315.0 5.5 %shard_map.113.rest_7_ = f32[512,4096]{1,0:T(8,128)} custom-call(s32[6]{0:T(128)} %copy-done.4, f32[128,4096]{1,0:T(8,128)} %collective-permute-done.15.base_ref.rest_2_, f32[512,4096]{1,0:T(8,128)} %get-tuple-element.61.before_ref), custom_call_target="tpu_custom_call", output_to_operand_aliasing={{}: (2, {})} | custom-call | flops 1000000 | bytes 65536 | tf_op jit(solution)/shard_map/pallas_call | solution.py:291
  320.5 9.5 %shard_map.114 = (f32[512,4096]{1,0:T(8,128)}, f32[32,4096]{1,0:T(8,128)}) custom-call(s32[3]{0:T(128)S(1)} %pad_add_fusion.3.at_ref, bf16[544,1024]{1,0:T(8,128)(2,1)S(1)} %get-tuple-element.69.high_ref, bf16[544,1024]{1,0:T(8,128)(2,1)S(1)} %get-tuple-element.68.low_ref, ...), custom_call_target="tpu_custom_call", output_to_operand_aliasing={{0}: (10, {}), {1}: (11, {})} | custom-call | flops 1000000 | bytes 65536 | tf_op jit(solution)/shard_map/pallas_call | solution.py:271
  (69 shorter events, 39.7 us)
Async XLA Ops:
  3.8 47.6 %collective-permute-start.3 = (f32[512,1024]{1,0:T(8,128)}, f32[512,1024]{1,0:T(8,128)S(1)}, u32[]{:S(2)}, u32[]{:S(2)}) collective-permute-start(f32[512,1024]{1,0:T(8,128)} %slice.37.refs_0_.rest_0_), channel_id=1, source_target_pairs={{0,4},{1,5},{6,2},{7,3},{4,6},{5,7},{2,0},{3,1},{8,12},{9,13},{14,... | collective-permute-start | bytes 6291464 | tf_op jit(solution)/shard_map/ppermute | solution.py:324
  5.1 51.4 %collective-permute-start.2 = (f32[512,1024]{1,0:T(8,128)}, f32[512,1024]{1,0:T(8,128)}, u32[]{:S(2)}, u32[]{:S(2)}) collective-permute-start(f32[512,1024]{1,0:T(8,128)} %slice.37.refs_0_.rest_0_), channel_id=1, source_target_pairs={{0,1},{1,0},{2,3},{3,2},{4,5},{5,4},{6,7},{7,6},{8,9},{9,8},{10,11... | collective-permute-start | bytes 6291464 | tf_op jit(solution)/shard_map/ppermute | solution.py:328
  13.2 50.9 %collective-permute-start = (f32[528,1024]{1,0:T(8,128)}, f32[528,1024]{1,0:T(8,128)}, u32[]{:S(2)}, u32[]{:S(2)}) collective-permute-start(f32[528,1024]{1,0:T(8,128)} %maximum_maximum_fusion), channel_id=1, source_target_pairs={{0,8},{8,16},{16,24},{1,9},{9,17},{17,25},{2,10},{10,18},{18,26},{... | collective-permute-start | bytes 6488072 | tf_op jit(solution)/shard_map/ppermute | solution.py:312
  51.4 67.9 %copy-start = (f32[512,1024]{1,0:T(8,128)}, f32[512,1024]{1,0:T(8,128)S(1)}, u32[]{:S(2)}) copy-start(f32[512,1024]{1,0:T(8,128)S(1)} %collective-permute-done.3.refs_2_.rest_2_) | copy-start | bytes 6291460
  54.2 45.7 %collective-permute-start.5 = (f32[512,1024]{1,0:T(8,128)S(1)}, f32[512,1024]{1,0:T(8,128)}, u32[]{:S(2)}, u32[]{:S(2)}) collective-permute-start(f32[512,1024]{1,0:T(8,128)S(1)} %broadcast_select_fusion.2), channel_id=1, source_target_pairs={{0,2},{1,3},{4,6},{5,7},{6,4},{7,5},{2,0},{3,1},{8,10},{9,11},{12,... | collective-permute-start | bytes 6291464 | tf_op jit(solution)/shard_map/ppermute | solution.py:324
  54.7 45.2 %collective-permute-start.4 = (f32[512,1024]{1,0:T(8,128)S(1)}, f32[512,1024]{1,0:T(8,128)S(1)}, u32[]{:S(2)}, u32[]{:S(2)}) collective-permute-start(f32[512,1024]{1,0:T(8,128)S(1)} %collective-permute-done.3.refs_2_.rest_2_), channel_id=1, source_target_pairs={{0,1},{1,0},{2,3},{3,2},{4,5},{5,4},{6,7},{7,6},{8,9},{9,8},{10,11... | collective-permute-start | bytes 6291464 | tf_op jit(solution)/shard_map/ppermute | solution.py:328
  56.5 49.5 %collective-permute-start.7 = (f32[512,1024]{1,0:T(8,128)}, f32[512,1024]{1,0:T(8,128)}, u32[]{:S(2)}, u32[]{:S(2)}) collective-permute-start(f32[512,1024]{1,0:T(8,128)} %slice.37.refs_0_.rest_0_), channel_id=1, source_target_pairs={{2,4},{3,5},{4,2},{5,3},{10,12},{11,13},{12,10},{13,11},{18,20},{1... | collective-permute-start | bytes 6291464 | tf_op jit(solution)/shard_map/ppermute | solution.py:324
  64.1 52.2 %collective-permute-start.1 = (f32[128,4096]{1,0:T(8,128)}, f32[128,4096]{1,0:T(8,128)}, u32[]{:S(2)}, u32[]{:S(2)}) collective-permute-start(f32[128,4096]{1,0:T(8,128)} %get-tuple-element.35), channel_id=1, source_target_pairs={{0,8},{8,16},{16,24},{1,9},{9,17},{17,25},{2,10},{10,18},{18,26},{... | collective-permute-start | bytes 6291464 | tf_op jit(solution)/shard_map/ppermute | solution.py:312
  101.2 18.1 %collective-permute-start.6 = (f32[512,1024]{1,0:T(8,128)}, f32[512,1024]{1,0:T(8,128)}, u32[]{:S(2)}, u32[]{:S(2)}) collective-permute-start(f32[512,1024]{1,0:T(8,128)} %collective-permute-done.5.refs_4_.rest_4_), channel_id=1, source_target_pairs={{0,1},{1,0},{2,3},{3,2},{4,5},{5,4},{6,7},{7,6},{8,9},{9,8},{10,11... | collective-permute-start | bytes 6291464 | tf_op jit(solution)/shard_map/ppermute | solution.py:328
  105.9 93.1 %collective-permute-start.8 = (f32[528,1024]{1,0:T(8,128)}, f32[528,1024]{1,0:T(8,128)}, u32[]{:S(2)}, u32[]{:S(2)}) collective-permute-start(f32[528,1024]{1,0:T(8,128)} %collective-permute-done.rest_2_), channel_id=1, source_target_pairs={{0,4},{1,5},{6,2},{7,3},{4,6},{5,7},{2,0},{3,1},{8,12},{9,13},{14,... | collective-permute-start | bytes 6488072 | tf_op jit(solution)/shard_map/ppermute | solution.py:324
  105.9 93.1 %collective-permute-start.9 = (f32[512,1024]{1,0:T(8,128)}, f32[512,1024]{1,0:T(8,128)}, u32[]{:S(2)}, u32[]{:S(2)}) collective-permute-start(f32[512,1024]{1,0:T(8,128)} %slice.37.refs_0_.rest_0_), channel_id=1, source_target_pairs={{2,6},{3,7},{4,0},{5,1},{10,14},{11,15},{12,8},{13,9},{18,22},{19,... | collective-permute-start | bytes 6291464 | tf_op jit(solution)/shard_map/ppermute | solution.py:324
  116.2 95.0 %collective-permute-start.11 = (f32[256,4096]{1,0:T(8,128)}, f32[256,4096]{1,0:T(8,128)}, u32[]{:S(2)}, u32[]{:S(2)}) collective-permute-start(f32[256,4096]{1,0:T(8,128)} %slice.43), channel_id=1, source_target_pairs={{0,8},{8,16},{16,24},{1,9},{9,17},{17,25},{2,10},{10,18},{18,26},{... | collective-permute-start | bytes 12582920 | tf_op jit(solution)/shard_map/ppermute | solution.py:312
  121.0 49.4 %copy-start.6 = (f32[512,1024]{1,0:T(8,128)S(1)}, f32[512,1024]{1,0:T(8,128)}, u32[]{:S(2)}) copy-start(f32[512,1024]{1,0:T(8,128)} %slice.38) | copy-start | bytes 6291460
  192.7 67.2 %collective-permute-start.12 = (f32[552,1024]{1,0:T(8,128)}, f32[552,1024]{1,0:T(8,128)}, u32[]{:S(2)}, u32[]{:S(2)}) collective-permute-start(f32[552,1024]{1,0:T(8,128)} %select_maximum_fusion), channel_id=1, source_target_pairs={{0,8},{8,16},{16,24},{1,9},{9,17},{17,25},{2,10},{10,18},{18,26},{... | collective-permute-start | bytes 6782984 | tf_op jit(solution)/shard_map/ppermute | solution.py:312
  202.7 57.2 %collective-permute-start.13 = (f32[528,1024]{1,0:T(8,128)}, f32[528,1024]{1,0:T(8,128)}, u32[]{:S(2)}, u32[]{:S(2)}) collective-permute-start(f32[528,1024]{1,0:T(8,128)} %broadcast_select_fusion), channel_id=1, source_target_pairs={{0,2},{1,3},{4,6},{5,7},{6,4},{7,5},{2,0},{3,1},{8,10},{9,11},{12,... | collective-permute-start | bytes 6488072 | tf_op jit(solution)/shard_map/ppermute | solution.py:324
  205.9 54.1 %collective-permute-start.14 = (f32[528,1024]{1,0:T(8,128)}, f32[528,1024]{1,0:T(8,128)}, u32[]{:S(2)}, u32[]{:S(2)}) collective-permute-start(f32[528,1024]{1,0:T(8,128)} %collective-permute-done.rest_2_), channel_id=1, source_target_pairs={{2,4},{3,5},{4,2},{5,3},{10,12},{11,13},{12,10},{13,11},{18,20},{1... | collective-permute-start | bytes 6488072 | tf_op jit(solution)/shard_map/ppermute | solution.py:324
  210.0 35.5 %collective-permute-start.10 = (f32[512,1024]{1,0:T(8,128)S(1)}, f32[512,1024]{1,0:T(8,128)}, u32[]{:S(2)}, u32[]{:S(2)}) collective-permute-start(f32[512,1024]{1,0:T(8,128)S(1)} %broadcast_select_fusion.1.rest_0_), channel_id=1, source_target_pairs={{0,1},{1,0},{2,3},{3,2},{4,5},{5,4},{6,7},{7,6},{8,9},{9,8},{10,11... | collective-permute-start | bytes 6291464 | tf_op jit(solution)/shard_map/ppermute | solution.py:328
  211.3 58.2 %collective-permute-start.18 = (f32[528,1024]{1,0:T(8,128)}, f32[528,1024]{1,0:T(8,128)}, u32[]{:S(2)}, u32[]{:S(2)}) collective-permute-start(f32[528,1024]{1,0:T(8,128)} %collective-permute-done.8.rest_4_), channel_id=1, source_target_pairs={{0,1},{1,0},{2,3},{3,2},{4,5},{5,4},{6,7},{7,6},{8,9},{9,8},{10,11... | collective-permute-start | bytes 6488072 | tf_op jit(solution)/shard_map/ppermute | solution.py:328
  259.9 9.9 %collective-permute-start.17 = (f32[528,1024]{1,0:T(8,128)}, f32[528,1024]{1,0:T(8,128)}, u32[]{:S(2)}, u32[]{:S(2)}) collective-permute-start(f32[528,1024]{1,0:T(8,128)} %collective-permute-done.rest_2_), channel_id=1, source_target_pairs={{0,1},{1,0},{2,3},{3,2},{4,5},{5,4},{6,7},{7,6},{8,9},{9,8},{10,11... | collective-permute-start | bytes 6488072 | tf_op jit(solution)/shard_map/ppermute | solution.py:328
  260.0 9.8 %collective-permute-start.19 = (f32[528,1024]{1,0:T(8,128)}, f32[528,1024]{1,0:T(8,128)}, u32[]{:S(2)}, u32[]{:S(2)}) collective-permute-start(f32[528,1024]{1,0:T(8,128)} %collective-permute-done.13.rest_6_), channel_id=1, source_target_pairs={{0,1},{1,0},{2,3},{3,2},{4,5},{5,4},{6,7},{7,6},{8,9},{9,8},{10,11... | collective-permute-start | bytes 6488072 | tf_op jit(solution)/shard_map/ppermute | solution.py:328
  260.5 52.1 %collective-permute-start.16 = (f32[528,1024]{1,0:T(8,128)}, f32[528,1024]{1,0:T(8,128)}, u32[]{:S(2)}, u32[]{:S(2)}) collective-permute-start(f32[528,1024]{1,0:T(8,128)} %collective-permute-done.rest_2_), channel_id=1, source_target_pairs={{2,6},{3,7},{4,0},{5,1},{10,14},{11,15},{12,8},{13,9},{18,22},{19,... | collective-permute-start | bytes 6488072 | tf_op jit(solution)/shard_map/ppermute | solution.py:324
  263.2 49.4 %collective-permute-start.15 = (f32[128,4096]{1,0:T(8,128)}, f32[128,4096]{1,0:T(8,128)}, u32[]{:S(2)}, u32[]{:S(2)}) collective-permute-start(f32[128,4096]{1,0:T(8,128)} %get-tuple-element.53), channel_id=1, source_target_pairs={{0,8},{8,16},{16,24},{1,9},{9,17},{17,25},{2,10},{10,18},{18,26},{... | collective-permute-start | bytes 6291464 | tf_op jit(solution)/shard_map/ppermute | solution.py:312
  269.4 51.1 %collective-permute-start.21 = (f32[528,1024]{1,0:T(8,128)}, f32[528,1024]{1,0:T(8,128)}, u32[]{:S(2)}, u32[]{:S(2)}) collective-permute-start(f32[528,1024]{1,0:T(8,128)} %collective-permute-done.14.rest_5_), channel_id=1, source_target_pairs={{0,1},{1,0},{2,3},{3,2},{4,5},{5,4},{6,7},{7,6},{8,9},{9,8},{10,11... | collective-permute-start | bytes 6488072 | tf_op jit(solution)/shard_map/ppermute | solution.py:328
  312.6 7.9 %collective-permute-start.20 = (f32[528,1024]{1,0:T(8,128)}, f32[528,1024]{1,0:T(8,128)}, u32[]{:S(2)}, u32[]{:S(2)}) collective-permute-start(f32[528,1024]{1,0:T(8,128)} %collective-permute-done.16.rest_3_), channel_id=1, source_target_pairs={{0,1},{1,0},{2,3},{3,2},{4,5},{5,4},{6,7},{7,6},{8,9},{9,8},{10,11... | collective-permute-start | bytes 6488072 | tf_op jit(solution)/shard_map/ppermute | solution.py:328
  (8 other events, 86.0 us)
